TPU v7x, 128 devices: a whole 4x4x4 slice. The times are simulated.
128 devices in a mesh: gx: 16 (over z, y), gy: 8 (over x, core).
Axes of the slice: x: 4, y: 4, z: 4, core: 2. Of those that a mesh axis runs over, the one named last changes fastest.
Arguments:
- centers: float32 [3, 262144], P(None, ('gx', 'gy')), may hold values from -6 to 6
- tilt_angle: float32 [262144], P(('gx', 'gy')), may hold values from -3.140625 to 3.140625
- turn_angle: float32 [262144], P(('gx', 'gy')), may hold values from -3.140625 to 3.140625
- radius: float32 [262144], P(('gx', 'gy')), may hold values from 0.5 to 2
- mobility_perp: float32 [262144], P(('gx', 'gy')), may hold values from 0.3 to 3
- mobility_axial: float32 [262144], P(('gx', 'gy')), may hold values from 0.2 to 2
- mobility_rot: float32 [262144], P(('gx', 'gy')), may hold values from 0.3 to 3
- external_load: float32 [6, 262144], P(None, ('gx', 'gy')), may hold values from -60 to 60
- local_first: int32 [327680], P(('gx', 'gy')), may hold values from 0 to 2047, as said below
- local_second: int32 [327680], P(('gx', 'gy')), may hold values from 0 to 2047
- arc_first: float32 [327680], P(('gx', 'gy')), may hold values from -1 to 1
- arc_second: float32 [327680], P(('gx', 'gy')), may hold values from -1 to 1
- cross_mine: int32 [128, 4, 256], P(('gx', 'gy')), may hold values from 0 to 2047
- cross_slot: int32 [128, 4, 256], P(('gx', 'gy')), may hold values from 0 to 127
- cross_arc_own: float32 [128, 4, 256], P(('gx', 'gy')), may hold values from -1 to 1
- cross_arc_other: float32 [128, 4, 256], P(('gx', 'gy')), may hold values from -1 to 1
- cross_count: int32 [128, 4], P(('gx', 'gy')), may hold values from 0 to 256, as said below
- export_rows: int32 [128, 4, 128], P(('gx', 'gy')), may hold values from 0 to 2047
Outputs:
- velocity: float32 [6, 262144], P(None, ('gx', 'gy'))
- force_local: float32 [327680], P(('gx', 'gy'))
- force_cross: float32 [128, 4, 256], P(('gx', 'gy'))
Inputs may be any that keep to these rules, and one draw needn't show every extreme that they name: local_second never equals local_first of the same pair. Slots c < cross_count[k, d] are live, the others dead. A direction whose partner lies outside the mesh has count 0. In every draw some block holds 256 live pairs.
All inputs are finite; a program needn't handle non-finite values.
Results may differ from a plain program's by a relative error of at most 0.00002.
Values sent between devices are 32-bit elements; how exact they have to be, the bound alone decides.
A program may use at most 64 MiB of HBM per device.

v0:
```python
import functools

import jax
import jax.numpy as jnp
from jax import lax
from jax.experimental import pallas as pl
from jax.experimental.pallas import tpu as pltpu
from jax.sharding import PartitionSpec as P


F32 = jnp.float32
I32 = jnp.int32
STEP_TIME = 0.5
FLOOR_GAP = 0.25
TINY = 1e-06
PARTS = 2
OFFSETS = ((0, 1), (1, 1), (1, 0), (1, -1))
MESH = pl.DeviceIdType.MESH
LOCAL_STARTS = (0, 8, 12)
CHUNKS = (
    [(0, s) for s in range(8)]
    + [(1, s) for s in range(8)]
    + [(2, s) for s in range(4, 8)]
    + [(3, s) for s in range(8)]
    + [(4, s) for s in range(8)]
    + [(5, s) for s in range(4, 8)]
    + [(6, s) for s in range(8)]
    + [(7, s) for s in range(8)]
)
LOCAL_CHUNKS = 40


def cross3(a, b):
    return [a[1] * b[2] - a[2] * b[1], a[2] * b[0] - a[0] * b[2], a[0] * b[1] - a[1] * b[0]]


def dot3(a, b):
    return a[0] * b[0] + a[1] * b[1] + a[2] * b[2]


def lanes_of(table, index):
    return jnp.take_along_axis(table, index, axis=1, mode="promise_in_bounds")


def kernel(
    n_gx,
    n_gy,
    h_cent,
    h_tilt,
    h_turn,
    h_rad,
    h_perp,
    h_axial,
    h_rot,
    h_load,
    h_lf,
    h_ls,
    h_a1,
    h_a2,
    h_mine,
    h_slot,
    h_own,
    h_oth,
    h_count,
    h_exp,
    o_vel,
    o_fl,
    o_fc,
    v_cent,
    v_tilt,
    v_turn,
    v_rad,
    v_perp,
    v_axial,
    v_rot,
    v_load,
    v_lf,
    v_ls,
    v_a1,
    v_a2,
    v_mine,
    v_slot,
    v_own,
    v_oth,
    s_count,
    v_exp,
    w_vel,
    w_fl,
    w_fc,
    t_seg,
    t_move,
    x_seg,
    pk,
    pk_int,
    key_hi,
    key_lo,
    push,
    a_mat,
    o_mat,
    send_s,
    recv_s,
    send_d,
    recv_d,
    send_e,
    recv_e,
    send_f,
    recv_f,
    send_g,
    recv_g,
    sum_a,
    got_a,
    sum_b,
    got_b,
    in_sem,
    out_sem,
    ex_send,
    ex_recv,
    a_send,
    a_recv,
    b_send,
    b_recv,
):
    gx = lax.axis_index("gx")
    gy = lax.axis_index("gy")

    def place(dx, dy):
        return (lax.rem(gx + (dx + n_gx), n_gx), lax.rem(gy + (dy + n_gy), n_gy))

    known = []
    for dx, dy in OFFSETS:
        known += [(dx % n_gx, dy % n_gy), (-dx % n_gx, -dy % n_gy)]
    known += [(0, o) for o in range(1, n_gy)] + [(o, 0) for o in range(1, n_gx)]
    known = list(dict.fromkeys(known))
    barrier = pltpu.get_barrier_semaphore()
    for dx, dy in known:
        pl.semaphore_signal(barrier, inc=1, device_id=place(dx, dy), device_id_type=MESH)

    sources = (h_cent, h_tilt, h_turn, h_rad, h_perp, h_axial, h_rot, h_load, h_lf, h_ls, h_a1, h_a2, h_mine, h_slot, h_own, h_oth, h_count, h_exp)
    targets = (v_cent, v_tilt, v_turn, v_rad, v_perp, v_axial, v_rot, v_load, v_lf, v_ls, v_a1, v_a2, v_mine, v_slot, v_own, v_oth, s_count, v_exp)
    loads_in = {}
    for i in (1, 2, 7, 4, 5, 6, 13, 15, 16, 17, 12, 14, 0, 3, 8, 9, 10, 11):
        loads_in[i] = pltpu.make_async_copy(sources[i], targets[i], in_sem.at[i])
        loads_in[i].start()

    def need(*which):
        for i in which:
            loads_in[i].wait()

    row8 = lax.broadcasted_iota(I32, (8, 128), 0)
    lane8 = lax.broadcasted_iota(I32, (8, 128), 1)
    heading8 = row8 // 2
    zero8 = jnp.zeros((8, 128), F32)

    def spread_rows(ref, row):
        return jnp.broadcast_to(ref[row : row + 1, :], (8, 128))

    need(1, 2)
    lifted = jnp.sin(v_tilt[...])
    tangent = [lifted * jnp.cos(v_turn[...]), lifted * jnp.sin(v_turn[...]), jnp.cos(v_tilt[...])]
    need(7, 4, 5, 6)
    for c in range(6):
        for r in range(16):
            x_seg[c, r : r + 1, :] = v_load[c : c + 1, r * 128 : (r + 1) * 128]

    def mobile(applied):
        along = dot3(tangent, applied)
        pulled = v_axial[...] * along
        return [v_perp[...] * applied[c] + pulled * tangent[c] for c in range(3)] + [
            v_rot[...] * applied[3 + c] for c in range(3)
        ]

    drift = mobile([x_seg[c] for c in range(6)])
    for c in range(3):
        t_seg[c] = tangent[c]
    for c in range(6):
        t_seg[3 + c] = drift[c]

    def unpacked(ref, into, field):
        for d in range(4):
            for h in range(2):
                into[field, 2 * d + h : 2 * d + h + 1, :] = ref[d : d + 1, h * 128 : (h + 1) * 128]
        return into[field]

    need(13, 15, 16)
    for d in range(4):
        for h in range(2):
            piece = slice(h * 128, (h + 1) * 128)
            send_s[d, h : h + 1, :] = v_slot[d : d + 1, piece].astype(F32)
            send_s[d, 2 + h : 3 + h, :] = v_oth[d : d + 1, piece]
    live_own = zero8
    for d in range(4):
        bound = s_count[0, d]
        live_own = jnp.where(
            (heading8 == d) & ((row8 - 2 * d) * 128 + lane8 < bound), 1.0, live_own
        )
    for d in range(4):
        send_s[d, 4:6, :] = live_own[2 * d : 2 * d + 2]

    pl.semaphore_wait(barrier, len(known))

    sent = []

    def remote(src, dst, step, d, to):
        copy = pltpu.make_async_remote_copy(
            src_ref=src,
            dst_ref=dst,
            send_sem=ex_send.at[step, d],
            recv_sem=ex_recv.at[step, d],
            device_id=to,
            device_id_type=MESH,
        )
        copy.start()
        sent.append(copy)
        return copy

    partner = [place(dx, dy) for dx, dy in OFFSETS]
    owner = [place(-dx, -dy) for dx, dy in OFFSETS]
    copies_s = [remote(send_s.at[d], recv_s.at[d], 0, d, partner[d]) for d in range(4)]

    need(0, 3)

    def table_row(c, r):
        if c < 3:
            return jnp.broadcast_to(v_cent[c : c + 1, r * 128 : (r + 1) * 128], (8, 128))
        if c == 3:
            return spread_rows(v_rad, r)
        return jnp.broadcast_to(t_seg[c - 4, r : r + 1, :], (8, 128))

    def move_row(c, r):
        return jnp.broadcast_to(t_move[c, r : r + 1, :], (8, 128))

    def picked(index, row_of, count):
        block = index >> 7
        lane = index & 127
        out = [None] * count
        for r in range(16):
            here = block == r
            for c in range(count):
                taken = lanes_of(row_of(c, r), lane)
                out[c] = taken if r == 0 else jnp.where(here, taken, out[c])
        return out

    def endpoint(values, arc):
        lever = [arc * values[4 + c] for c in range(3)]
        place_of = [values[c] + lever[c] for c in range(3)]
        turned = cross3(values[10:13], lever)
        moving = [values[7 + c] + turned[c] for c in range(3)]
        return dict(lever=lever, at=place_of, radius=values[3], moving=moving)

    need(17)
    exports = v_exp[...]
    offered = picked(jnp.concatenate([exports, exports], axis=0), table_row, 13)
    for d in range(4):
        for c in range(13):
            send_e[d, c : c + 1, :] = offered[c][d : d + 1]
    copies_e = [remote(send_e.at[d], recv_e.at[d], 1, d, owner[d]) for d in range(4)]

    need(12, 14)
    index = [None] * 8
    index[6] = unpacked(v_mine, pk_int, 0)
    arc_own = unpacked(v_own, pk, 1)
    own = endpoint(picked(index[6], table_row, 13), arc_own)
    for i, value in enumerate(own["at"] + [own["radius"]] + own["moving"]):
        for d in range(4):
            send_d[d, 2 * i : 2 * i + 2, :] = value[2 * d : 2 * d + 2]
    copies_d = [remote(send_d.at[d], recv_d.at[d], 2, d, partner[d]) for d in range(4)]

    def pair(one, two, live):
        apart = [one["at"][c] - two["at"][c] for c in range(3)]
        spacing = jnp.sqrt(dot3(apart, apart))
        scale = 1.0 / jnp.maximum(spacing, FLOOR_GAP)
        if live is not None:
            scale = scale * live
        normal = [a * scale for a in apart]
        clearance = spacing - one["radius"] - two["radius"]
        if live is not None:
            clearance = clearance * live
        rate = dot3(normal, [one["moving"][c] - two["moving"][c] for c in range(3)])
        slope = clearance * (1.0 / STEP_TIME) + rate
        return dict(normal=normal, slope=slope, down=jnp.maximum(0.0, -slope))

    def split(value):
        pieces = []
        for _ in range(PARTS):
            piece = value.astype(jnp.bfloat16).astype(F32)
            pieces.append(piece)
            value = value - piece
        return pieces

    def set_keys(e):
        key_hi[e] = (index[e] >> 7) & 7
        key_lo[e] = ((index[e] >> 10) << 7) | (index[e] & 127)

    def set_push(e, first, normal, arm, amounts):
        sign = 1.0 if first else -1.0
        for i, amount in enumerate(amounts):
            scaled = amount * sign
            for c in range(6):
                value = scaled * (normal[c] if c < 3 else arm[c - 3])
                for p, piece in enumerate(split(value)):
                    push[p * 6 * len(amounts) + i * 6 + c, e] = piece

    def set_columns(chunks, start):
        low = lax.broadcasted_iota(I32, (256, 128), 0)
        for n, (e, s) in enumerate(chunks):
            at = (start + n) * 128
            key = jnp.broadcast_to(key_lo[e, s : s + 1, :], (256, 128))
            o_mat[:, at : at + 128] = jnp.where(low == key, 1.0, 0.0).astype(jnp.bfloat16)

    def set_rows(chunks, start, count):
        for n, (e, s) in enumerate(chunks):
            at = (start + n) * 128
            here = row8 == jnp.broadcast_to(key_hi[e, s : s + 1, :], (8, 128))
            for k in range(0, count, 2):
                two = [
                    jnp.where(here, jnp.broadcast_to(push[k + j, e, s : s + 1, :], (8, 128)), 0.0)
                    for j in range(2)
                ]
                a_mat[k * 8 : k * 8 + 16, at : at + 128] = jnp.concatenate(two, axis=0).astype(jnp.bfloat16)

    def summed(start, chunks, count):
        cols = slice(start * 128, (start + chunks) * 128)
        return lax.dot_general(
            a_mat[0 : count * 8, cols],
            o_mat[:, cols],
            (((1,), (1,)), ((), ())),
            preferred_element_type=F32,
        )

    def loads_of(total, groups):
        out = []
        for i in range(groups * 6):
            value = None
            for p in reversed(range(PARTS)):
                at = (p * 6 * groups + i) * 8
                piece = jnp.concatenate(
                    [total[at : at + 8, 0:128], total[at : at + 8, 128:256]], axis=0
                )
                value = piece if value is None else value + piece
            out.append(value)
        return out

    need(8, 9, 10, 11)
    pairs = [None] * 5
    ends = [None] * 8
    for b, start in enumerate(LOCAL_STARTS):
        index[b] = v_lf[start : start + 8, :]
        index[3 + b] = v_ls[start : start + 8, :]
        ends[b] = endpoint(picked(index[b], table_row, 13), v_a1[start : start + 8, :])
        ends[3 + b] = endpoint(picked(index[3 + b], table_row, 13), v_a2[start : start + 8, :])
        pairs[b] = pair(ends[b], ends[3 + b], None)
    ends[6] = own

    def set_ends(b, one, two, amounts):
        if one is not None:
            set_push(one, True, pairs[b]["normal"], cross3(ends[one]["lever"], pairs[b]["normal"]), amounts)
        if two is not None:
            set_push(two, False, pairs[b]["normal"], cross3(ends[two]["lever"], pairs[b]["normal"]), amounts)

    wide = 12 * PARTS
    narrow = 6 * PARTS
    for b in range(3):
        set_keys(b)
        set_keys(3 + b)
        set_ends(b, b, 3 + b, (pairs[b]["slope"], pairs[b]["down"]))
    set_keys(6)
    set_columns(CHUNKS[:48], 0)
    set_rows(CHUNKS[:LOCAL_CHUNKS], 0, wide)
    total = summed(0, LOCAL_CHUNKS, wide)

    for copy in copies_s:
        copy.wait_recv()

    def repacked(ref, field, slot):
        for d in range(4):
            pk[slot, 2 * d : 2 * d + 2, :] = ref[d, 2 * field : 2 * field + 2, :]
        return pk[slot]

    def by_heading(row_of):
        out = row_of(0)
        for d in range(1, 4):
            out = jnp.where(heading8 == d, row_of(d), out)
        return out

    slot_in = repacked(recv_s, 0, 2).astype(I32)
    arc_in = repacked(recv_s, 1, 3)
    live_in = repacked(recv_s, 2, 4)
    index[7] = lanes_of(by_heading(lambda d: spread_rows(v_exp, d)), slot_in)
    ends[7] = endpoint(picked(index[7], table_row, 13), arc_in)
    set_keys(7)
    set_columns(CHUNKS[48:], 48)

    slot_own = unpacked(v_slot, pk_int, 1)
    arc_oth = unpacked(v_oth, pk, 6)
    for copy in copies_e:
        copy.wait_recv()
    far = [
        lanes_of(
            by_heading(lambda d, c=c: jnp.broadcast_to(recv_e[d, c : c + 1, :], (8, 128))), slot_own
        )
        for c in range(13)
    ]
    pairs[3] = pair(own, endpoint(far, arc_oth), live_own)
    set_ends(3, 6, None, (pairs[3]["slope"], pairs[3]["down"]))
    for copy in copies_d:
        copy.wait_recv()
    near = [repacked(recv_d, i, 7 + i) for i in range(7)]
    pairs[4] = pair(dict(at=near[0:3], radius=near[3], moving=near[4:7]), ends[7], live_in)
    set_ends(4, None, 7, (pairs[4]["slope"], pairs[4]["down"]))

    set_rows(CHUNKS[LOCAL_CHUNKS:], LOCAL_CHUNKS, wide)
    total = total + summed(LOCAL_CHUNKS, len(CHUNKS) - LOCAL_CHUNKS, wide)
    both = loads_of(total, 2)
    moved_all = mobile(both[0:6])
    moved_down = mobile(both[6:12])
    for c in range(6):
        t_move[c] = moved_down[c]

    def folded(value):
        return jnp.sum(value, axis=0, keepdims=True)

    def halved(row):
        row = row + pltpu.roll(row, 64, 1)
        return row + pltpu.roll(row, 32, 1)

    def counted(name):
        value = pairs[0][name] * pairs[0][name] + pairs[1][name] * pairs[1][name]
        last = pairs[2][name] * pairs[2][name]
        return value + jnp.where(row8 >= 4, last, 0.0) + pairs[3][name] * pairs[3][name]

    def power(one, two):
        value = one[0] * two[0]
        for c in range(1, 6):
            value = value + one[c] * two[c]
        return value

    rows = [
        halved(folded(v))
        for v in (counted("slope"), power(both[0:6], moved_all), counted("down"), power(both[6:12], moved_down))
    ]
    quarter = lax.broadcasted_iota(I32, (1, 128), 1) // 32
    mine = rows[0]
    for i in range(1, 4):
        mine = jnp.where(quarter == i, rows[i], mine)
    sum_a[...] = mine

    def ring(src, dst, send, recv, o, to):
        copy = pltpu.make_async_remote_copy(
            src_ref=src,
            dst_ref=dst.at[o - 1],
            send_sem=send.at[o - 1],
            recv_sem=recv.at[o - 1],
            device_id=to,
            device_id_type=MESH,
        )
        copy.start()
        sent.append(copy)
        return copy

    copies_a = [ring(sum_a, got_a, a_send, a_recv, o, place(0, o)) for o in range(1, n_gy)]

    def contact(e):
        values = picked(index[e], move_row, 6)
        turned = cross3(values[3:6], ends[e]["lever"])
        return [values[c] + turned[c] for c in range(3)]

    moved_own = contact(6)
    for c in range(3):
        for d in range(4):
            send_f[d, 2 * c : 2 * c + 2, :] = moved_own[c][2 * d : 2 * d + 2]
    copies_f = [remote(send_f.at[d], recv_f.at[d], 3, d, partner[d]) for d in range(4)]
    moved_in = contact(7)
    for c in range(3):
        for d in range(4):
            send_g[d, 2 * c : 2 * c + 2, :] = moved_in[c][2 * d : 2 * d + 2]
    copies_g = [remote(send_g.at[d], recv_g.at[d], 4, d, owner[d]) for d in range(4)]

    for copy in copies_a:
        copy.wait_recv()
    mine = sum_a[...]
    for o in range(1, n_gy):
        mine = mine + got_a[o - 1]
    sum_b[...] = mine
    copies_b = [ring(sum_b, got_b, b_send, b_recv, o, place(o, 0)) for o in range(1, n_gx)]

    def curve(b, one, two):
        return dot3(pairs[b]["normal"], [one[c] - two[c] for c in range(3)])

    curved = [None] * 5
    for b in range(3):
        curved[b] = curve(b, contact(b), contact(3 + b))
    for copy in copies_f + copies_g:
        copy.wait_recv()
    curved[3] = curve(3, moved_own, [repacked(recv_g, c, c) for c in range(3)])
    curved[4] = curve(4, [repacked(recv_f, c, 3 + c) for c in range(3)], moved_in)

    for copy in copies_b:
        copy.wait_recv()
    mine = sum_b[...]
    for o in range(1, n_gx):
        mine = mine + got_b[o - 1]
    sums = [
        jnp.sum(jnp.where(quarter == i, mine, 0.0), axis=1, keepdims=True) for i in range(4)
    ]
    step_first = sums[0] / (sums[1] + TINY)
    square = step_first * step_first
    step_second = (square * sums[2]) / (square * sums[3] + TINY)
    step_first = jnp.broadcast_to(step_first, (8, 128))
    step_second = jnp.broadcast_to(step_second, (8, 128))

    force = []
    for b in range(5):
        thrust = step_first * pairs[b]["down"]
        slope = pairs[b]["slope"] + step_first * curved[b]
        force.append(jnp.maximum(0.0, thrust - step_second * slope))
    for b, start in enumerate(LOCAL_STARTS):
        w_fl[start : start + 8, :] = force[b]
    for d in range(4):
        for h in range(2):
            w_fc[d : d + 1, h * 128 : (h + 1) * 128] = force[3][2 * d + h : 2 * d + h + 1]
    out_fl = pltpu.make_async_copy(w_fl, o_fl, out_sem.at[0])
    out_fl.start()
    out_fc = pltpu.make_async_copy(w_fc, o_fc, out_sem.at[1])
    out_fc.start()
    for b in range(3):
        set_ends(b, b, 3 + b, (force[b],))
    set_ends(3, 6, None, (force[3],))
    set_ends(4, None, 7, (force[4],))
    set_rows(CHUNKS, 0, narrow)
    moved = mobile(loads_of(summed(0, len(CHUNKS), narrow), 1))
    for c in range(6):
        velocity = t_seg[3 + c] + moved[c]
        for r in range(16):
            w_vel[c : c + 1, r * 128 : (r + 1) * 128] = velocity[r : r + 1]
    out_vel = pltpu.make_async_copy(w_vel, o_vel, out_sem.at[2])
    out_vel.start()
    for copy in sent:
        copy.wait_send()
    out_fl.wait()
    out_fc.wait()
    out_vel.wait()


def on_device(n_gx, n_gy, cent, tilt, turn, rad, perp, axial, rot, load, lf, ls, a1, a2, mine, slot, own, oth, count, exports):
    segs = [v.reshape(16, 128) for v in (tilt, turn, rad, perp, axial, rot)]
    local = [v.reshape(20, 128) for v in (lf, ls, a1, a2)]
    cross = [v.reshape(4, 256) for v in (mine, slot, own, oth)]
    operands = [cent, *segs, load, *local, *cross, count, exports.reshape(4, 128)]
    anyspace = pl.BlockSpec(memory_space=pltpu.HBM)

    def held(v):
        return pltpu.VMEM(v.shape, v.dtype)

    inputs = [held(v) for v in operands]
    inputs[16] = pltpu.SMEM(count.shape, count.dtype)
    dma = pltpu.SemaphoreType.DMA
    scratch = inputs + [
        pltpu.VMEM((6, 2048), F32),
        pltpu.VMEM((20, 128), F32),
        pltpu.VMEM((4, 256), F32),
        pltpu.VMEM((9, 16, 128), F32),
        pltpu.VMEM((6, 16, 128), F32),
        pltpu.VMEM((6, 16, 128), F32),
        pltpu.VMEM((14, 8, 128), F32),
        pltpu.VMEM((2, 8, 128), I32),
        pltpu.VMEM((8, 8, 128), I32),
        pltpu.VMEM((8, 8, 128), I32),
        pltpu.VMEM((12 * PARTS, 8, 8, 128), F32),
        pltpu.VMEM((96 * PARTS, 128 * len(CHUNKS)), jnp.bfloat16),
        pltpu.VMEM((256, 128 * len(CHUNKS)), jnp.bfloat16),
        pltpu.VMEM((4, 8, 128), F32),
        pltpu.VMEM((4, 8, 128), F32),
        pltpu.VMEM((4, 16, 128), F32),
        pltpu.VMEM((4, 16, 128), F32),
        pltpu.VMEM((4, 16, 128), F32),
        pltpu.VMEM((4, 16, 128), F32),
        pltpu.VMEM((4, 8, 128), F32),
        pltpu.VMEM((4, 8, 128), F32),
        pltpu.VMEM((4, 8, 128), F32),
        pltpu.VMEM((4, 8, 128), F32),
        pltpu.VMEM((1, 128), F32),
        pltpu.VMEM((n_gy - 1, 1, 128), F32),
        pltpu.VMEM((1, 128), F32),
        pltpu.VMEM((n_gx - 1, 1, 128), F32),
        dma((18,)),
        dma((3,)),
        dma((5, 4)),
        dma((5, 4)),
        dma((n_gy - 1,)),
        dma((n_gy - 1,)),
        dma((n_gx - 1,)),
        dma((n_gx - 1,)),
    ]
    velocity, force_local, force_cross = pl.pallas_call(
        functools.partial(kernel, n_gx, n_gy),
        out_shape=(
            jax.ShapeDtypeStruct((6, 2048), F32),
            jax.ShapeDtypeStruct((20, 128), F32),
            jax.ShapeDtypeStruct((4, 256), F32),
        ),
        in_specs=[anyspace] * 18,
        out_specs=(anyspace,) * 3,
        scratch_shapes=scratch,
        compiler_params=pltpu.CompilerParams(
            collective_id=0, has_side_effects=True, vmem_limit_bytes=67_043_328
        ),
    )(*operands)
    return velocity, force_local.reshape(2560), force_cross.reshape(1, 4, 256)


def solution(mesh):
    both = ("gx", "gy")
    flat = P(both)
    wide = P(None, both)
    cube = P(both, None, None)
    return jax.shard_map(
        functools.partial(on_device, mesh.shape["gx"], mesh.shape["gy"]),
        mesh=mesh,
        in_specs=(wide, *[flat] * 6, wide, *[flat] * 4, *[cube] * 4, P(both, None), cube),
        out_specs=(wide, flat, cube),
        check_vma=False,
    )
```

profile of v0, /device:TPU:1, one launch (start us, length us, event | category | flops | bytes accessed | tf_op | source)
XLA Modules:
  0.0 30.3 jit_solution(17820507823970748835)
XLA Ops:
  0.6 26.9 %shard_map.193 = (f32[6,2048]{1,0:T(8,128)}, f32[20,128]{1,0:T(8,128)}, f32[4,256]{1,0:T(4,128)}) custom-call(f32[3,2048]{1,0:T(4,128)} %h_cent.1, f32[16,128]{1,0:T(8,128)} %bitcast.22, f32[16,128]{1,0:T(8,128)} %bitcast.23, f32[16,128]{1,0:T(8,128)} %bitcast.24, f32[16,128]{1,0:T(8,128)} %bitcast.25, f32[16,128]{1,0:T(8,128)} %bitcast.26, ...), custom_call_target="tpu_custom_call" | custom-call | tf_op jit(solution)/shard_map/pallas_call | solution.py:594
  27.6 0.0 copy-start
  27.6 1.5 %copy.24 = f32[6,2048]{1,0:T(8,128)} copy(f32[6,2048]{1,0:T(8,128)} %get-tuple-element.12) | data formatting | bytes 98304
  29.0 0.0 copy-done
  29.0 0.0 copy-start.1
  29.0 0.6 %copy.25 = f32[2560]{0:T(1024)} copy(f32[2560]{0:T(1024)S(1)} %bitcast.17) | data formatting | bytes 20480
  29.6 0.1 copy-done.1
  29.7 0.6 %copy.26 = f32[1,4,256]{2,1,0:T(4,128)} copy(f32[1,4,256]{2,1,0:T(4,128)S(1)} %bitcast.28) | data formatting | bytes 8192
Async XLA Ops:
  27.6 1.5 %copy-start = (f32[20,128]{1,0:T(8,128)S(1)}, f32[20,128]{1,0:T(8,128)}, u32[]{:S(2)}) copy-start(f32[20,128]{1,0:T(8,128)} %get-tuple-element.7) | copy-start | bytes 30724
  29.0 0.7 %copy-start.1 = (f32[4,256]{1,0:T(4,128)S(1)}, f32[4,256]{1,0:T(4,128)}, u32[]{:S(2)}) copy-start(f32[4,256]{1,0:T(4,128)} %get-tuple-element.8) | copy-start | bytes 12292
where the time goes:
time: 30.5 us; the launch traced here: 30.3 us
  Pallas kernels  26.9 us (88%)
  local copies, waits for them, and re-layouts  2.75 us (9%)
  between operations  0.66 us (2%)
    pallas_call x1, Pallas kernels, on_device(): pl.pallas_call(functools.partial(kernel, n_gx, n_gy), out_shape=(jax.Shap...  26.9 us
    unnamed x7, local copies, waits for them, and re-layouts  2.75 us

commit v1 on v0

--- a/solution.py
+++ b/solution.py
@@ -84,9 +84,6 @@
     v_oth,
     s_count,
     v_exp,
-    w_vel,
-    w_fl,
-    w_fc,
     t_seg,
     t_move,
     x_seg,
@@ -95,8 +92,8 @@
     key_hi,
     key_lo,
     push,
-    a_mat,
     o_mat,
+    acc,
     send_s,
     recv_s,
     send_d,
@@ -112,13 +109,13 @@
     sum_b,
     got_b,
     in_sem,
-    out_sem,
     ex_send,
     ex_recv,
     a_send,
     a_recv,
     b_send,
     b_recv,
+    relay,
 ):
     gx = lax.axis_index("gx")
     gy = lax.axis_index("gy")
@@ -126,14 +123,19 @@
     def place(dx, dy):
         return (lax.rem(gx + (dx + n_gx), n_gx), lax.rem(gy + (dy + n_gy), n_gy))
 
-    known = []
-    for dx, dy in OFFSETS:
-        known += [(dx % n_gx, dy % n_gy), (-dx % n_gx, -dy % n_gy)]
-    known += [(0, o) for o in range(1, n_gy)] + [(o, 0) for o in range(1, n_gx)]
-    known = list(dict.fromkeys(known))
-    barrier = pltpu.get_barrier_semaphore()
-    for dx, dy in known:
-        pl.semaphore_signal(barrier, inc=1, device_id=place(dx, dy), device_id_type=MESH)
+    n_y = grid_y(n_gx)
+    n_z = n_gx // n_y
+    at_y, at_z = lax.rem(gx, n_y), gx // n_y
+
+    def plane(oy, oz):
+        return (lax.rem(at_z + oz, n_z) * n_y + lax.rem(at_y + oy, n_y), gy)
+
+    def inside(dx, dy):
+        row, column = gx + dx, gy + dy
+        return (row >= 0) & (row < n_gx) & (column >= 0) & (column < n_gy)
+
+    has_partner = [inside(dx, dy) for dx, dy in OFFSETS]
+    has_owner = [inside(-dx, -dy) for dx, dy in OFFSETS]
 
     sources = (h_cent, h_tilt, h_turn, h_rad, h_perp, h_axial, h_rot, h_load, h_lf, h_ls, h_a1, h_a2, h_mine, h_slot, h_own, h_oth, h_count, h_exp)
     targets = (v_cent, v_tilt, v_turn, v_rad, v_perp, v_axial, v_rot, v_load, v_lf, v_ls, v_a1, v_a2, v_mine, v_slot, v_own, v_oth, s_count, v_exp)
@@ -142,6 +144,24 @@
         loads_in[i] = pltpu.make_async_copy(sources[i], targets[i], in_sem.at[i])
         loads_in[i].start()
 
+    barrier = pltpu.get_barrier_semaphore()
+
+    def greet(to):
+        pl.semaphore_signal(barrier, inc=1, device_id=to, device_id_type=MESH)
+
+    greetings = (n_gy - 1) + (n_y - 1) + (n_z - 1)
+    for d in (1, 2, 3):
+        dx, dy = OFFSETS[d]
+        pl.when(has_partner[d])(functools.partial(greet, place(dx, dy)))
+        pl.when(has_owner[d])(functools.partial(greet, place(-dx, -dy)))
+        greetings = greetings + has_partner[d].astype(I32) + has_owner[d].astype(I32)
+    for o in range(1, n_gy):
+        greet(place(0, o))
+    for o in range(1, n_y):
+        greet(plane(o, 0))
+    for o in range(1, n_z):
+        greet(plane(0, o))
+
     def need(*which):
         for i in which:
             loads_in[i].wait()
@@ -151,8 +171,8 @@
     heading8 = row8 // 2
     zero8 = jnp.zeros((8, 128), F32)
 
-    def spread_rows(ref, row):
-        return jnp.broadcast_to(ref[row : row + 1, :], (8, 128))
+    def spread_rows(ref, row, *lead):
+        return ref[(*lead, pl.ds(row, 8, stride=0), slice(None))]
 
     need(1, 2)
     lifted = jnp.sin(v_tilt[...])
@@ -196,38 +216,59 @@
     for d in range(4):
         send_s[d, 4:6, :] = live_own[2 * d : 2 * d + 2]
 
-    pl.semaphore_wait(barrier, len(known))
-
-    sent = []
-
-    def remote(src, dst, step, d, to):
-        copy = pltpu.make_async_remote_copy(
-            src_ref=src,
-            dst_ref=dst,
-            send_sem=ex_send.at[step, d],
-            recv_sem=ex_recv.at[step, d],
-            device_id=to,
-            device_id_type=MESH,
-        )
-        copy.start()
-        sent.append(copy)
-        return copy
+    def blank(refs, d):
+        for ref in refs:
+            ref[d] = jnp.zeros(ref.shape[1:], F32)
+
+    for d in range(4):
+        pl.when(~has_partner[d])(functools.partial(blank, (recv_e, recv_g), d))
+        pl.when(~has_owner[d])(functools.partial(blank, (recv_s, recv_d, recv_f), d))
+
+    pl.semaphore_wait(barrier, greetings)
+    for o in range(1, n_z):
+        pl.semaphore_signal(relay.at[0], inc=1, device_id=plane(0, o), device_id_type=MESH)
 
     partner = [place(dx, dy) for dx, dy in OFFSETS]
     owner = [place(-dx, -dy) for dx, dy in OFFSETS]
-    copies_s = [remote(send_s.at[d], recv_s.at[d], 0, d, partner[d]) for d in range(4)]
+    moves = {}
+
+    def launch(src, dst, step, to_partner):
+        moves[step] = to_partner, []
+        for d in range(4):
+            copy = pltpu.make_async_remote_copy(
+                src_ref=src.at[d],
+                dst_ref=dst.at[d],
+                send_sem=ex_send.at[step, d],
+                recv_sem=ex_recv.at[step, d],
+                device_id=partner[d] if to_partner else owner[d],
+                device_id_type=MESH,
+            )
+            moves[step][1].append(copy)
+            pl.when(has_partner[d] if to_partner else has_owner[d])(copy.start)
+
+    def arrive(step):
+        to_partner, copies = moves[step]
+        for d in range(4):
+            pl.when(has_owner[d] if to_partner else has_partner[d])(copies[d].wait_recv)
+
+    launch(send_s, recv_s, 0, True)
 
     need(0, 3)
+    for c in range(3):
+        for r in range(16):
+            t_seg[9 + c, r : r + 1, :] = v_cent[c : c + 1, r * 128 : (r + 1) * 128]
 
     def table_row(c, r):
         if c < 3:
-            return jnp.broadcast_to(v_cent[c : c + 1, r * 128 : (r + 1) * 128], (8, 128))
+            return spread_rows(t_seg, r, 9 + c)
         if c == 3:
             return spread_rows(v_rad, r)
-        return jnp.broadcast_to(t_seg[c - 4, r : r + 1, :], (8, 128))
+        return spread_rows(t_seg, r, c - 4)
 
     def move_row(c, r):
-        return jnp.broadcast_to(t_move[c, r : r + 1, :], (8, 128))
+        return spread_rows(t_move, r, c)
+
+    beside = []
 
     def picked(index, row_of, count):
         block = index >> 7
@@ -238,6 +279,8 @@
             for c in range(count):
                 taken = lanes_of(row_of(c, r), lane)
                 out[c] = taken if r == 0 else jnp.where(here, taken, out[c])
+            if beside:
+                beside.pop(0)()
         return out
 
     def endpoint(values, arc):
@@ -253,7 +296,7 @@
     for d in range(4):
         for c in range(13):
             send_e[d, c : c + 1, :] = offered[c][d : d + 1]
-    copies_e = [remote(send_e.at[d], recv_e.at[d], 1, d, owner[d]) for d in range(4)]
+    launch(send_e, recv_e, 1, False)
 
     need(12, 14)
     index = [None] * 8
@@ -263,7 +306,7 @@
     for i, value in enumerate(own["at"] + [own["radius"]] + own["moving"]):
         for d in range(4):
             send_d[d, 2 * i : 2 * i + 2, :] = value[2 * d : 2 * d + 2]
-    copies_d = [remote(send_d.at[d], recv_d.at[d], 2, d, partner[d]) for d in range(4)]
+    launch(send_d, recv_d, 2, True)
 
     def pair(one, two, live):
         apart = [one["at"][c] - two["at"][c] for c in range(3)]
@@ -288,8 +331,18 @@
         return pieces
 
     def set_keys(e):
-        key_hi[e] = (index[e] >> 7) & 7
-        key_lo[e] = ((index[e] >> 10) << 7) | (index[e] & 127)
+        key_hi[e] = ((index[e] >> 7) & 7).astype(F32)
+        key_lo[e] = (((index[e] >> 10) << 7) | (index[e] & 127)).astype(F32)
+
+    def tall_row(first, second):
+        return jnp.concatenate([first, second], axis=0).astype(jnp.bfloat16)
+
+    low = [
+        tall_row(row8.astype(F32) + float(k), row8.astype(F32) + float(k + 8)) for k in range(0, 256, 16)
+    ]
+    high = tall_row(row8.astype(F32), row8.astype(F32))
+    one16 = jnp.ones((16, 128), jnp.bfloat16)
+    none16 = jnp.zeros((16, 128), jnp.bfloat16)
 
     def set_push(e, first, normal, arm, amounts):
         sign = 1.0 if first else -1.0
@@ -298,44 +351,47 @@
             for c in range(6):
                 value = scaled * (normal[c] if c < 3 else arm[c - 3])
                 for p, piece in enumerate(split(value)):
-                    push[p * 6 * len(amounts) + i * 6 + c, e] = piece
-
-    def set_columns(chunks, start):
-        low = lax.broadcasted_iota(I32, (256, 128), 0)
-        for n, (e, s) in enumerate(chunks):
-            at = (start + n) * 128
-            key = jnp.broadcast_to(key_lo[e, s : s + 1, :], (256, 128))
-            o_mat[:, at : at + 128] = jnp.where(low == key, 1.0, 0.0).astype(jnp.bfloat16)
-
-    def set_rows(chunks, start, count):
-        for n, (e, s) in enumerate(chunks):
-            at = (start + n) * 128
-            here = row8 == jnp.broadcast_to(key_hi[e, s : s + 1, :], (8, 128))
-            for k in range(0, count, 2):
-                two = [
-                    jnp.where(here, jnp.broadcast_to(push[k + j, e, s : s + 1, :], (8, 128)), 0.0)
-                    for j in range(2)
-                ]
-                a_mat[k * 8 : k * 8 + 16, at : at + 128] = jnp.concatenate(two, axis=0).astype(jnp.bfloat16)
-
-    def summed(start, chunks, count):
-        cols = slice(start * 128, (start + chunks) * 128)
+                    push[(i * PARTS + p) * 6 + c, e] = piece
+
+    def set_columns(n):
+        e, s = CHUNKS[n]
+        key = spread_rows(key_lo, s, e)
+        key = tall_row(key, key)
+        for k in range(0, 256, 16):
+            o_mat[n, k : k + 16, :] = jnp.where(low[k // 16] == key, one16, none16)
+
+    def columns_beside(first, last, every):
+        for n in range(first, last):
+            beside.append(functools.partial(set_columns, n))
+            beside.extend([lambda: None] * (every - 1))
+
+    def loads_from(chunk, count):
+        e, s = chunk
+        key = spread_rows(key_hi, s, e)
+        here = high == tall_row(key, key)
+        out = []
+        for k in range(0, count, 2):
+            value = tall_row(spread_rows(push, s, k, e), spread_rows(push, s, k + 1, e))
+            out.append(jnp.where(here, value, none16))
+        return out
+
+    def product(start, rows, group):
+        tiles = 3 * PARTS
+        left = [jnp.concatenate(r[group * tiles : (group + 1) * tiles], axis=0) for r in rows]
         return lax.dot_general(
-            a_mat[0 : count * 8, cols],
-            o_mat[:, cols],
+            jnp.concatenate(left, axis=1),
+            jnp.concatenate([o_mat[start + n] for n in range(len(rows))], axis=1),
             (((1,), (1,)), ((), ())),
             preferred_element_type=F32,
         )
 
-    def loads_of(total, groups):
+    def loads_of(total):
         out = []
-        for i in range(groups * 6):
+        for c in range(6):
             value = None
             for p in reversed(range(PARTS)):
-                at = (p * 6 * groups + i) * 8
-                piece = jnp.concatenate(
-                    [total[at : at + 8, 0:128], total[at : at + 8, 128:256]], axis=0
-                )
+                at = (p * 6 + c) * 8
+                piece = jnp.concatenate([total[at : at + 8, 0:128], total[at : at + 8, 128:256]], axis=0)
                 value = piece if value is None else value + piece
             out.append(value)
         return out
@@ -346,6 +402,11 @@
     for b, start in enumerate(LOCAL_STARTS):
         index[b] = v_lf[start : start + 8, :]
         index[3 + b] = v_ls[start : start + 8, :]
+        set_keys(b)
+        set_keys(3 + b)
+    set_keys(6)
+    columns_beside(0, 48, 2)
+    for b, start in enumerate(LOCAL_STARTS):
         ends[b] = endpoint(picked(index[b], table_row, 13), v_a1[start : start + 8, :])
         ends[3 + b] = endpoint(picked(index[3 + b], table_row, 13), v_a2[start : start + 8, :])
         pairs[b] = pair(ends[b], ends[3 + b], None)
@@ -360,16 +421,12 @@
     wide = 12 * PARTS
     narrow = 6 * PARTS
     for b in range(3):
-        set_keys(b)
-        set_keys(3 + b)
         set_ends(b, b, 3 + b, (pairs[b]["slope"], pairs[b]["down"]))
-    set_keys(6)
-    set_columns(CHUNKS[:48], 0)
-    set_rows(CHUNKS[:LOCAL_CHUNKS], 0, wide)
-    total = summed(0, LOCAL_CHUNKS, wide)
-
-    for copy in copies_s:
-        copy.wait_recv()
+    rows = [loads_from(chunk, wide) for chunk in CHUNKS[:LOCAL_CHUNKS]]
+    for group in range(2):
+        acc[group] = product(0, rows, group)
+
+    arrive(0)
 
     def repacked(ref, field, slot):
         for d in range(4):
@@ -386,31 +443,30 @@
     arc_in = repacked(recv_s, 1, 3)
     live_in = repacked(recv_s, 2, 4)
     index[7] = lanes_of(by_heading(lambda d: spread_rows(v_exp, d)), slot_in)
+    set_keys(7)
+    columns_beside(48, 56, 2)
     ends[7] = endpoint(picked(index[7], table_row, 13), arc_in)
-    set_keys(7)
-    set_columns(CHUNKS[48:], 48)
 
     slot_own = unpacked(v_slot, pk_int, 1)
     arc_oth = unpacked(v_oth, pk, 6)
-    for copy in copies_e:
-        copy.wait_recv()
+    arrive(1)
     far = [
         lanes_of(
-            by_heading(lambda d, c=c: jnp.broadcast_to(recv_e[d, c : c + 1, :], (8, 128))), slot_own
+            by_heading(lambda d, c=c: spread_rows(recv_e, c, d)), slot_own
         )
         for c in range(13)
     ]
     pairs[3] = pair(own, endpoint(far, arc_oth), live_own)
     set_ends(3, 6, None, (pairs[3]["slope"], pairs[3]["down"]))
-    for copy in copies_d:
-        copy.wait_recv()
+    arrive(2)
     near = [repacked(recv_d, i, 7 + i) for i in range(7)]
     pairs[4] = pair(dict(at=near[0:3], radius=near[3], moving=near[4:7]), ends[7], live_in)
     set_ends(4, None, 7, (pairs[4]["slope"], pairs[4]["down"]))
 
-    set_rows(CHUNKS[LOCAL_CHUNKS:], LOCAL_CHUNKS, wide)
-    total = total + summed(LOCAL_CHUNKS, len(CHUNKS) - LOCAL_CHUNKS, wide)
-    both = loads_of(total, 2)
+    rows = [loads_from(chunk, wide) for chunk in CHUNKS[LOCAL_CHUNKS:]]
+    both = []
+    for group in range(2):
+        both += loads_of(acc[group] + product(LOCAL_CHUNKS, rows, group))
     moved_all = mobile(both[0:6])
     moved_down = mobile(both[6:12])
     for c in range(6):
@@ -444,20 +500,28 @@
         mine = jnp.where(quarter == i, rows[i], mine)
     sum_a[...] = mine
 
-    def ring(src, dst, send, recv, o, to):
-        copy = pltpu.make_async_remote_copy(
+    def ring(src, dst, sems, slot, to):
+        return pltpu.make_async_remote_copy(
             src_ref=src,
-            dst_ref=dst.at[o - 1],
-            send_sem=send.at[o - 1],
-            recv_sem=recv.at[o - 1],
+            dst_ref=dst.at[slot],
+            send_sem=sems[0].at[0],
+            recv_sem=sems[1].at[0],
             device_id=to,
             device_id_type=MESH,
         )
-        copy.start()
-        sent.append(copy)
-        return copy
-
-    copies_a = [ring(sum_a, got_a, a_send, a_recv, o, place(0, o)) for o in range(1, n_gy)]
+
+    def whole(dst, sems):
+        return pltpu.make_async_remote_copy(
+            src_ref=dst,
+            dst_ref=dst,
+            send_sem=sems[0].at[0],
+            recv_sem=sems[1].at[0],
+            device_id=place(0, 1),
+            device_id_type=MESH,
+        )
+
+    for o in range(1, n_gy):
+        ring(sum_a, got_a, (a_send, a_recv), o - 1, place(0, o)).start()
 
     def contact(e):
         values = picked(index[e], move_row, 6)
@@ -468,20 +532,21 @@
     for c in range(3):
         for d in range(4):
             send_f[d, 2 * c : 2 * c + 2, :] = moved_own[c][2 * d : 2 * d + 2]
-    copies_f = [remote(send_f.at[d], recv_f.at[d], 3, d, partner[d]) for d in range(4)]
+    launch(send_f, recv_f, 3, True)
     moved_in = contact(7)
     for c in range(3):
         for d in range(4):
             send_g[d, 2 * c : 2 * c + 2, :] = moved_in[c][2 * d : 2 * d + 2]
-    copies_g = [remote(send_g.at[d], recv_g.at[d], 4, d, owner[d]) for d in range(4)]
-
-    for copy in copies_a:
-        copy.wait_recv()
+    launch(send_g, recv_g, 4, False)
+
+    whole(got_a, (a_send, a_recv)).wait_recv()
     mine = sum_a[...]
     for o in range(1, n_gy):
         mine = mine + got_a[o - 1]
     sum_b[...] = mine
-    copies_b = [ring(sum_b, got_b, b_send, b_recv, o, place(o, 0)) for o in range(1, n_gx)]
+    pl.semaphore_wait(relay.at[0], n_z - 1)
+    for o in range(1, n_gx):
+        ring(sum_b, got_b, (b_send, b_recv), o - 1, plane(o % n_y, o // n_y)).start()
 
     def curve(b, one, two):
         return dot3(pairs[b]["normal"], [one[c] - two[c] for c in range(3)])
@@ -489,13 +554,12 @@
     curved = [None] * 5
     for b in range(3):
         curved[b] = curve(b, contact(b), contact(3 + b))
-    for copy in copies_f + copies_g:
-        copy.wait_recv()
+    arrive(3)
+    arrive(4)
     curved[3] = curve(3, moved_own, [repacked(recv_g, c, c) for c in range(3)])
     curved[4] = curve(4, [repacked(recv_f, c, 3 + c) for c in range(3)], moved_in)
 
-    for copy in copies_b:
-        copy.wait_recv()
+    whole(got_b, (b_send, b_recv)).wait_recv()
     mine = sum_b[...]
     for o in range(1, n_gx):
         mine = mine + got_b[o - 1]
@@ -514,31 +578,43 @@
         slope = pairs[b]["slope"] + step_first * curved[b]
         force.append(jnp.maximum(0.0, thrust - step_second * slope))
     for b, start in enumerate(LOCAL_STARTS):
-        w_fl[start : start + 8, :] = force[b]
+        o_fl[start : start + 8, :] = force[b]
     for d in range(4):
         for h in range(2):
-            w_fc[d : d + 1, h * 128 : (h + 1) * 128] = force[3][2 * d + h : 2 * d + h + 1]
-    out_fl = pltpu.make_async_copy(w_fl, o_fl, out_sem.at[0])
-    out_fl.start()
-    out_fc = pltpu.make_async_copy(w_fc, o_fc, out_sem.at[1])
-    out_fc.start()
+            o_fc[d : d + 1, h * 128 : (h + 1) * 128] = force[3][2 * d + h : 2 * d + h + 1]
     for b in range(3):
         set_ends(b, b, 3 + b, (force[b],))
     set_ends(3, 6, None, (force[3],))
     set_ends(4, None, 7, (force[4],))
-    set_rows(CHUNKS, 0, narrow)
-    moved = mobile(loads_of(summed(0, len(CHUNKS), narrow), 1))
+    half = len(CHUNKS) // 2
+    rows = [loads_from(chunk, narrow) for chunk in CHUNKS]
+    acc[0] = product(0, rows[:half], 0)
+    acc[1] = product(half, rows[half:], 0)
+    moved = mobile(loads_of(acc[0] + acc[1]))
     for c in range(6):
         velocity = t_seg[3 + c] + moved[c]
         for r in range(16):
-            w_vel[c : c + 1, r * 128 : (r + 1) * 128] = velocity[r : r + 1]
-    out_vel = pltpu.make_async_copy(w_vel, o_vel, out_sem.at[2])
-    out_vel.start()
-    for copy in sent:
-        copy.wait_send()
-    out_fl.wait()
-    out_fc.wait()
-    out_vel.wait()
+            o_vel[c : c + 1, r * 128 : (r + 1) * 128] = velocity[r : r + 1]
+    whole(got_a, (a_send, a_recv)).wait_send()
+    whole(got_b, (b_send, b_recv)).wait_send()
+    for to_partner, copies in moves.values():
+        for d in range(4):
+            pl.when(has_partner[d] if to_partner else has_owner[d])(copies[d].wait_send)
+
+
+def hand_out(vel, fl, fc, o_vel, o_fl, o_fc, sem):
+    copies = [
+        pltpu.make_async_copy(src, dst, sem.at[i])
+        for i, (src, dst) in enumerate(((vel, o_vel), (fl, o_fl), (fc, o_fc)))
+    ]
+    for copy in copies:
+        copy.start()
+    for copy in copies:
+        copy.wait()
+
+
+def grid_y(n_gx):
+    return max(k for k in range(1, n_gx + 1) if n_gx % k == 0 and k * k <= n_gx)
 
 
 def on_device(n_gx, n_gy, cent, tilt, turn, rad, perp, axial, rot, load, lf, ls, a1, a2, mine, slot, own, oth, count, exports):
@@ -555,19 +631,16 @@
     inputs[16] = pltpu.SMEM(count.shape, count.dtype)
     dma = pltpu.SemaphoreType.DMA
     scratch = inputs + [
-        pltpu.VMEM((6, 2048), F32),
-        pltpu.VMEM((20, 128), F32),
-        pltpu.VMEM((4, 256), F32),
-        pltpu.VMEM((9, 16, 128), F32),
+        pltpu.VMEM((12, 16, 128), F32),
         pltpu.VMEM((6, 16, 128), F32),
         pltpu.VMEM((6, 16, 128), F32),
         pltpu.VMEM((14, 8, 128), F32),
         pltpu.VMEM((2, 8, 128), I32),
-        pltpu.VMEM((8, 8, 128), I32),
-        pltpu.VMEM((8, 8, 128), I32),
+        pltpu.VMEM((8, 8, 128), F32),
+        pltpu.VMEM((8, 8, 128), F32),
         pltpu.VMEM((12 * PARTS, 8, 8, 128), F32),
-        pltpu.VMEM((96 * PARTS, 128 * len(CHUNKS)), jnp.bfloat16),
-        pltpu.VMEM((256, 128 * len(CHUNKS)), jnp.bfloat16),
+        pltpu.VMEM((len(CHUNKS), 256, 128), jnp.bfloat16),
+        pltpu.VMEM((2, 48 * PARTS, 256), F32),
         pltpu.VMEM((4, 8, 128), F32),
         pltpu.VMEM((4, 8, 128), F32),
         pltpu.VMEM((4, 16, 128), F32),
@@ -583,28 +656,35 @@
         pltpu.VMEM((1, 128), F32),
         pltpu.VMEM((n_gx - 1, 1, 128), F32),
         dma((18,)),
-        dma((3,)),
         dma((5, 4)),
         dma((5, 4)),
-        dma((n_gy - 1,)),
-        dma((n_gy - 1,)),
-        dma((n_gx - 1,)),
-        dma((n_gx - 1,)),
+        dma((1,)),
+        dma((1,)),
+        dma((1,)),
+        dma((1,)),
+        pltpu.SemaphoreType.REGULAR((1,)),
     ]
-    velocity, force_local, force_cross = pl.pallas_call(
+    operands = [pltpu.with_memory_space_constraint(v, pltpu.HBM) for v in operands]
+    outs = ((6, 2048), (20, 128), (4, 256))
+    near = pl.BlockSpec(memory_space=pltpu.VMEM)
+    solved = pl.pallas_call(
         functools.partial(kernel, n_gx, n_gy),
-        out_shape=(
-            jax.ShapeDtypeStruct((6, 2048), F32),
-            jax.ShapeDtypeStruct((20, 128), F32),
-            jax.ShapeDtypeStruct((4, 256), F32),
-        ),
+        out_shape=tuple(pltpu.VMEM(shape, F32) for shape in outs),
         in_specs=[anyspace] * 18,
-        out_specs=(anyspace,) * 3,
+        out_specs=(near,) * 3,
         scratch_shapes=scratch,
         compiler_params=pltpu.CompilerParams(
-            collective_id=0, has_side_effects=True, vmem_limit_bytes=67_043_328
+            collective_id=0, has_side_effects=True, vmem_limit_bytes=48 * 1024 * 1024
         ),
     )(*operands)
+    velocity, force_local, force_cross = pl.pallas_call(
+        hand_out,
+        out_shape=tuple(jax.ShapeDtypeStruct(shape, F32) for shape in outs),
+        in_specs=[near] * 3,
+        out_specs=(anyspace,) * 3,
+        scratch_shapes=[dma((3,))],
+        compiler_params=pltpu.CompilerParams(vmem_limit_bytes=1024 * 1024),
+    )(*[pltpu.with_memory_space_constraint(v, pltpu.VMEM) for v in solved])
     return velocity, force_local.reshape(2560), force_cross.reshape(1, 4, 256)
 
 

time: 30.5 us -> 25 us (0.82)
  Pallas kernels: 26.9 us -> 24 us
  local copies, waits for them, and re-layouts: 2.75 us -> 0 us
    pallas_call x1 -> x2, Pallas kernels: 26.9 us -> 24 us  [the longest x1 23.3 us: on_device(): pl.pallas_call(functools.partial(kernel, n_gx, n_gy), out_shape=tuple((pl...]
    unnamed x7 -> x0, local copies, waits for them, and re-layouts: 2.75 us -> none
where the time goes in v1:
time: 25 us; the launch traced here: 24.6 us
  Pallas kernels  24 us (96%)
  between operations  0.65 us (3%)
    pallas_call x1, Pallas kernels, on_device(): pl.pallas_call(functools.partial(kernel, n_gx, n_gy), out_shape=tuple((pl...  23.3 us
    pallas_call x1, Pallas kernels, on_device(): pl.pallas_call(hand_out, out_shape=tuple((jax.ShapeDtypeStruct(shape, F32...  0.66 us

profile of v1, /device:TPU:1, one launch (start us, length us, event | category | flops | bytes accessed | tf_op | source)
XLA Modules:
  0.0 24.6 jit_solution(8259499617807371723)
XLA Ops:
  0.6 23.3 %shard_map.193 = (f32[6,2048]{1,0:T(8,128)S(1)}, f32[20,128]{1,0:T(8,128)S(1)}, f32[4,256]{1,0:T(4,128)S(1)}) custom-call(f32[3,2048]{1,0:T(4,128)} %h_cent.1, f32[16,128]{1,0:T(8,128)} %bitcast.21, f32[16,128]{1,0:T(8,128)} %bitcast.22, f32[16,128]{1,0:T(8,128)} %bitcast.23, f32[16,128]{1,0:T(8,128)} %bitcast.24, f32[16,128]{1,0:T(8,128)} %bitcast.25, ...), custom_call_target="tpu_custom_call" | custom-call | tf_op jit(solution)/shard_map/pallas_call | solution.py:670
  24.0 0.7 %shard_map.194 = (f32[6,2048]{1,0:T(8,128)}, f32[20,128]{1,0:T(8,128)}, f32[4,256]{1,0:T(4,128)}) custom-call(f32[6,2048]{1,0:T(8,128)S(1)} %get-tuple-element.9.vel, f32[20,128]{1,0:T(8,128)S(1)} %get-tuple-element.10.fl, f32[4,256]{1,0:T(4,128)S(1)} %get-tuple-element.11.fc), custom_call_target="tpu_custom_call" | custom-call | tf_op jit(solution)/shard_map/pallas_call | solution.py:680

commit v2 on v1

--- a/solution.py
+++ b/solution.py
@@ -93,7 +93,6 @@
     key_lo,
     push,
     o_mat,
-    acc,
     send_s,
     recv_s,
     send_d,
@@ -116,6 +115,10 @@
     b_send,
     b_recv,
     relay,
+    wide_0,
+    wide_1,
+    narrow_0,
+    narrow_1,
 ):
     gx = lax.axis_index("gx")
     gy = lax.axis_index("gy")
@@ -375,22 +378,28 @@
             out.append(jnp.where(here, value, none16))
         return out
 
-    def product(start, rows, group):
-        tiles = 3 * PARTS
-        left = [jnp.concatenate(r[group * tiles : (group + 1) * tiles], axis=0) for r in rows]
-        return lax.dot_general(
-            jnp.concatenate(left, axis=1),
-            jnp.concatenate([o_mat[start + n] for n in range(len(rows))], axis=1),
-            (((1,), (1,)), ((), ())),
-            preferred_element_type=F32,
-        )
-
-    def loads_of(total):
+    def accumulate(into, start, rows):
+        for n in range(0, len(rows), 2):
+            unit = (start + n) // 2 % 2
+            stage = (start + n) // 4 % 2
+            pltpu.matmul_push_rhs(
+                jnp.concatenate([o_mat[start + n], o_mat[start + n + 1]], axis=1),
+                staging_register=stage,
+                mxu_index=unit,
+                transpose=True,
+            )
+            left = [jnp.concatenate(r, axis=0) for r in rows[n : n + 2]]
+            pltpu.matmul_acc_lhs(into[unit], jnp.concatenate(left, axis=1), load_staged_rhs=stage)
+
+    def total_of(into):
+        return pltpu.matmul_pop(into[0]) + pltpu.matmul_pop(into[1])
+
+    def loads_of(total, group):
         out = []
         for c in range(6):
             value = None
             for p in reversed(range(PARTS)):
-                at = (p * 6 + c) * 8
+                at = ((group * PARTS + p) * 6 + c) * 8
                 piece = jnp.concatenate([total[at : at + 8, 0:128], total[at : at + 8, 128:256]], axis=0)
                 value = piece if value is None else value + piece
             out.append(value)
@@ -422,9 +431,8 @@
     narrow = 6 * PARTS
     for b in range(3):
         set_ends(b, b, 3 + b, (pairs[b]["slope"], pairs[b]["down"]))
-    rows = [loads_from(chunk, wide) for chunk in CHUNKS[:LOCAL_CHUNKS]]
-    for group in range(2):
-        acc[group] = product(0, rows, group)
+    both_units = (wide_0, wide_1)
+    accumulate(both_units, 0, [loads_from(chunk, wide) for chunk in CHUNKS[:LOCAL_CHUNKS]])
 
     arrive(0)
 
@@ -463,10 +471,9 @@
     pairs[4] = pair(dict(at=near[0:3], radius=near[3], moving=near[4:7]), ends[7], live_in)
     set_ends(4, None, 7, (pairs[4]["slope"], pairs[4]["down"]))
 
-    rows = [loads_from(chunk, wide) for chunk in CHUNKS[LOCAL_CHUNKS:]]
-    both = []
-    for group in range(2):
-        both += loads_of(acc[group] + product(LOCAL_CHUNKS, rows, group))
+    accumulate(both_units, LOCAL_CHUNKS, [loads_from(chunk, wide) for chunk in CHUNKS[LOCAL_CHUNKS:]])
+    total = total_of(both_units)
+    both = loads_of(total, 0) + loads_of(total, 1)
     moved_all = mobile(both[0:6])
     moved_down = mobile(both[6:12])
     for c in range(6):
@@ -586,11 +593,9 @@
         set_ends(b, b, 3 + b, (force[b],))
     set_ends(3, 6, None, (force[3],))
     set_ends(4, None, 7, (force[4],))
-    half = len(CHUNKS) // 2
-    rows = [loads_from(chunk, narrow) for chunk in CHUNKS]
-    acc[0] = product(0, rows[:half], 0)
-    acc[1] = product(half, rows[half:], 0)
-    moved = mobile(loads_of(acc[0] + acc[1]))
+    both_units = (narrow_0, narrow_1)
+    accumulate(both_units, 0, [loads_from(chunk, narrow) for chunk in CHUNKS])
+    moved = mobile(loads_of(total_of(both_units), 0))
     for c in range(6):
         velocity = t_seg[3 + c] + moved[c]
         for r in range(16):
@@ -600,6 +605,11 @@
     for to_partner, copies in moves.values():
         for d in range(4):
             pl.when(has_partner[d] if to_partner else has_owner[d])(copies[d].wait_send)
+
+
+def kernel_with_sums(*refs):
+    sums = [pltpu.ACC(unit)((rows * PARTS, 256), F32) for rows in (96, 48) for unit in range(2)]
+    pl.run_scoped(functools.partial(kernel, *refs), *sums)
 
 
 def hand_out(vel, fl, fc, o_vel, o_fl, o_fc, sem):
@@ -640,7 +650,6 @@
         pltpu.VMEM((8, 8, 128), F32),
         pltpu.VMEM((12 * PARTS, 8, 8, 128), F32),
         pltpu.VMEM((len(CHUNKS), 256, 128), jnp.bfloat16),
-        pltpu.VMEM((2, 48 * PARTS, 256), F32),
         pltpu.VMEM((4, 8, 128), F32),
         pltpu.VMEM((4, 8, 128), F32),
         pltpu.VMEM((4, 16, 128), F32),
@@ -668,7 +677,7 @@
     outs = ((6, 2048), (20, 128), (4, 256))
     near = pl.BlockSpec(memory_space=pltpu.VMEM)
     solved = pl.pallas_call(
-        functools.partial(kernel, n_gx, n_gy),
+        functools.partial(kernel_with_sums, n_gx, n_gy),
         out_shape=tuple(pltpu.VMEM(shape, F32) for shape in outs),
         in_specs=[anyspace] * 18,
         out_specs=(near,) * 3,

time: 25 us -> 23.3 us (0.932)
  Pallas kernels: 24 us -> 22.3 us
    pallas_call x1, Pallas kernels: 23.3 us -> 21.6 us  [on_device(): pl.pallas_call(functools.partial(kernel_with_sums, n_gx, n_gy), out_shape...]
where the time goes in v2:
time: 23.3 us; the launch traced here: 23 us
  Pallas kernels  22.3 us (96%)
  between operations  0.65 us (3%)
    pallas_call x1, Pallas kernels, on_device(): pl.pallas_call(functools.partial(kernel_with_sums, n_gx, n_gy), out_shape...  21.6 us
    pallas_call x1, Pallas kernels, on_device(): pl.pallas_call(hand_out, out_shape=tuple((jax.ShapeDtypeStruct(shape, F32...  0.66 us

profile of v2, /device:TPU:1, one launch (start us, length us, event | category | flops | bytes accessed | tf_op | source)
XLA Modules:
  0.0 23.0 jit_solution(4952479168133934786)
XLA Ops:
  0.6 21.6 %shard_map.193 = (f32[6,2048]{1,0:T(8,128)S(1)}, f32[20,128]{1,0:T(8,128)S(1)}, f32[4,256]{1,0:T(4,128)S(1)}) custom-call(f32[3,2048]{1,0:T(4,128)} %refs_0_.1, f32[16,128]{1,0:T(8,128)} %bitcast.21, f32[16,128]{1,0:T(8,128)} %bitcast.22, f32[16,128]{1,0:T(8,128)} %bitcast.23, f32[16,128]{1,0:T(8,128)} %bitcast.24, f32[16,128]{1,0:T(8,128)} %bitcast.25, ...), custom_call_target="tpu_custom_call" | custom-call | tf_op jit(solution)/shard_map/pallas_call | solution.py:679
  22.3 0.7 %shard_map.194 = (f32[6,2048]{1,0:T(8,128)}, f32[20,128]{1,0:T(8,128)}, f32[4,256]{1,0:T(4,128)}) custom-call(f32[6,2048]{1,0:T(8,128)S(1)} %get-tuple-element.9.vel, f32[20,128]{1,0:T(8,128)S(1)} %get-tuple-element.10.fl, f32[4,256]{1,0:T(4,128)S(1)} %get-tuple-element.11.fc), custom_call_target="tpu_custom_call" | custom-call | tf_op jit(solution)/shard_map/pallas_call | solution.py:689

commit v3 on v2

--- a/solution.py
+++ b/solution.py
@@ -28,6 +28,7 @@
     + [(7, s) for s in range(8)]
 )
 LOCAL_CHUNKS = 40
+EARLY = 48
 
 
 def cross3(a, b):
@@ -93,8 +94,10 @@
     key_lo,
     push,
     o_mat,
-    send_s,
-    recv_s,
+    o_turned,
+    key_rows,
+    key_columns,
+    turned,
     send_d,
     recv_d,
     send_e,
@@ -208,8 +211,8 @@
     for d in range(4):
         for h in range(2):
             piece = slice(h * 128, (h + 1) * 128)
-            send_s[d, h : h + 1, :] = v_slot[d : d + 1, piece].astype(F32)
-            send_s[d, 2 + h : 3 + h, :] = v_oth[d : d + 1, piece]
+            send_d[d, 16 + h : 17 + h, :] = v_slot[d : d + 1, piece].astype(F32)
+            send_d[d, 18 + h : 19 + h, :] = v_oth[d : d + 1, piece]
     live_own = zero8
     for d in range(4):
         bound = s_count[0, d]
@@ -217,7 +220,7 @@
             (heading8 == d) & ((row8 - 2 * d) * 128 + lane8 < bound), 1.0, live_own
         )
     for d in range(4):
-        send_s[d, 4:6, :] = live_own[2 * d : 2 * d + 2]
+        send_d[d, 20:22, :] = live_own[2 * d : 2 * d + 2]
 
     def blank(refs, d):
         for ref in refs:
@@ -225,11 +228,7 @@
 
     for d in range(4):
         pl.when(~has_partner[d])(functools.partial(blank, (recv_e, recv_g), d))
-        pl.when(~has_owner[d])(functools.partial(blank, (recv_s, recv_d, recv_f), d))
-
-    pl.semaphore_wait(barrier, greetings)
-    for o in range(1, n_z):
-        pl.semaphore_signal(relay.at[0], inc=1, device_id=plane(0, o), device_id_type=MESH)
+        pl.when(~has_owner[d])(functools.partial(blank, (recv_d, recv_f), d))
 
     partner = [place(dx, dy) for dx, dy in OFFSETS]
     owner = [place(-dx, -dy) for dx, dy in OFFSETS]
@@ -254,7 +253,6 @@
         for d in range(4):
             pl.when(has_owner[d] if to_partner else has_partner[d])(copies[d].wait_recv)
 
-    launch(send_s, recv_s, 0, True)
 
     need(0, 3)
     for c in range(3):
@@ -299,7 +297,6 @@
     for d in range(4):
         for c in range(13):
             send_e[d, c : c + 1, :] = offered[c][d : d + 1]
-    launch(send_e, recv_e, 1, False)
 
     need(12, 14)
     index = [None] * 8
@@ -309,7 +306,12 @@
     for i, value in enumerate(own["at"] + [own["radius"]] + own["moving"]):
         for d in range(4):
             send_d[d, 2 * i : 2 * i + 2, :] = value[2 * d : 2 * d + 2]
-    launch(send_d, recv_d, 2, True)
+    pl.semaphore_wait(barrier, greetings)
+    for o in range(1, n_z):
+        pl.semaphore_signal(relay.at[0], inc=1, device_id=plane(0, o), device_id_type=MESH)
+
+    launch(send_e, recv_e, 0, False)
+    launch(send_d, recv_d, 1, True)
 
     def pair(one, two, live):
         apart = [one["at"][c] - two["at"][c] for c in range(3)]
@@ -356,12 +358,28 @@
                 for p, piece in enumerate(split(value)):
                     push[(i * PARTS + p) * 6 + c, e] = piece
 
+    lanes = [
+        tall_row((lane8 + 128 * h).astype(F32), (lane8 + 128 * h).astype(F32)) for h in range(2)
+    ]
+
+    def turn_keys():
+        for n, (e, s) in enumerate(CHUNKS[:EARLY]):
+            key_rows[n : n + 1, :] = key_lo[e, s : s + 1, :]
+        key_rows[EARLY:, :] = jnp.zeros((128 - EARLY, 128), F32)
+        key_columns[...] = jnp.transpose(key_rows[...])
+
     def set_columns(n):
+        if n < EARLY:
+            for k in range(0, 128, 16):
+                key = jnp.broadcast_to(key_columns[k : k + 16, n : n + 1], (16, 128)).astype(jnp.bfloat16)
+                for h in range(2):
+                    o_turned[n, h, k : k + 16, :] = jnp.where(lanes[h] == key, one16, none16)
+            return
         e, s = CHUNKS[n]
         key = spread_rows(key_lo, s, e)
         key = tall_row(key, key)
         for k in range(0, 256, 16):
-            o_mat[n, k : k + 16, :] = jnp.where(low[k // 16] == key, one16, none16)
+            o_mat[n - EARLY, k : k + 16, :] = jnp.where(low[k // 16] == key, one16, none16)
 
     def columns_beside(first, last, every):
         for n in range(first, last):
@@ -382,11 +400,17 @@
         for n in range(0, len(rows), 2):
             unit = (start + n) // 2 % 2
             stage = (start + n) // 4 % 2
+            if start + n < EARLY:
+                tile = [
+                    jnp.concatenate([o_turned[at, 0], o_turned[at, 1]], axis=1)
+                    for at in (start + n, start + n + 1)
+                ]
+                tile = jnp.concatenate(tile, axis=0)
+            else:
+                at = start + n - EARLY
+                tile = jnp.concatenate([o_mat[at], o_mat[at + 1]], axis=1)
             pltpu.matmul_push_rhs(
-                jnp.concatenate([o_mat[start + n], o_mat[start + n + 1]], axis=1),
-                staging_register=stage,
-                mxu_index=unit,
-                transpose=True,
+                tile, staging_register=stage, mxu_index=unit, transpose=start + n >= EARLY
             )
             left = [jnp.concatenate(r, axis=0) for r in rows[n : n + 2]]
             pltpu.matmul_acc_lhs(into[unit], jnp.concatenate(left, axis=1), load_staged_rhs=stage)
@@ -414,7 +438,8 @@
         set_keys(b)
         set_keys(3 + b)
     set_keys(6)
-    columns_beside(0, 48, 2)
+    turn_keys()
+    columns_beside(0, EARLY, 2)
     for b, start in enumerate(LOCAL_STARTS):
         ends[b] = endpoint(picked(index[b], table_row, 13), v_a1[start : start + 8, :])
         ends[3 + b] = endpoint(picked(index[3 + b], table_row, 13), v_a2[start : start + 8, :])
@@ -435,6 +460,7 @@
     accumulate(both_units, 0, [loads_from(chunk, wide) for chunk in CHUNKS[:LOCAL_CHUNKS]])
 
     arrive(0)
+    arrive(1)
 
     def repacked(ref, field, slot):
         for d in range(4):
@@ -447,17 +473,16 @@
             out = jnp.where(heading8 == d, row_of(d), out)
         return out
 
-    slot_in = repacked(recv_s, 0, 2).astype(I32)
-    arc_in = repacked(recv_s, 1, 3)
-    live_in = repacked(recv_s, 2, 4)
+    slot_in = repacked(recv_d, 8, 2).astype(I32)
+    arc_in = repacked(recv_d, 9, 3)
+    live_in = repacked(recv_d, 10, 4)
     index[7] = lanes_of(by_heading(lambda d: spread_rows(v_exp, d)), slot_in)
     set_keys(7)
-    columns_beside(48, 56, 2)
+    columns_beside(EARLY, len(CHUNKS), 2)
     ends[7] = endpoint(picked(index[7], table_row, 13), arc_in)
 
     slot_own = unpacked(v_slot, pk_int, 1)
     arc_oth = unpacked(v_oth, pk, 6)
-    arrive(1)
     far = [
         lanes_of(
             by_heading(lambda d, c=c: spread_rows(recv_e, c, d)), slot_own
@@ -466,7 +491,6 @@
     ]
     pairs[3] = pair(own, endpoint(far, arc_oth), live_own)
     set_ends(3, 6, None, (pairs[3]["slope"], pairs[3]["down"]))
-    arrive(2)
     near = [repacked(recv_d, i, 7 + i) for i in range(7)]
     pairs[4] = pair(dict(at=near[0:3], radius=near[3], moving=near[4:7]), ends[7], live_in)
     set_ends(4, None, 7, (pairs[4]["slope"], pairs[4]["down"]))
@@ -539,12 +563,12 @@
     for c in range(3):
         for d in range(4):
             send_f[d, 2 * c : 2 * c + 2, :] = moved_own[c][2 * d : 2 * d + 2]
-    launch(send_f, recv_f, 3, True)
+    launch(send_f, recv_f, 2, True)
     moved_in = contact(7)
     for c in range(3):
         for d in range(4):
             send_g[d, 2 * c : 2 * c + 2, :] = moved_in[c][2 * d : 2 * d + 2]
-    launch(send_g, recv_g, 4, False)
+    launch(send_g, recv_g, 3, False)
 
     whole(got_a, (a_send, a_recv)).wait_recv()
     mine = sum_a[...]
@@ -561,8 +585,8 @@
     curved = [None] * 5
     for b in range(3):
         curved[b] = curve(b, contact(b), contact(3 + b))
+    arrive(2)
     arrive(3)
-    arrive(4)
     curved[3] = curve(3, moved_own, [repacked(recv_g, c, c) for c in range(3)])
     curved[4] = curve(4, [repacked(recv_f, c, 3 + c) for c in range(3)], moved_in)
 
@@ -598,8 +622,10 @@
     moved = mobile(loads_of(total_of(both_units), 0))
     for c in range(6):
         velocity = t_seg[3 + c] + moved[c]
-        for r in range(16):
-            o_vel[c : c + 1, r * 128 : (r + 1) * 128] = velocity[r : r + 1]
+        for j in range(2):
+            turned[j, c * 8 : c * 8 + 8, :] = velocity[j * 8 : j * 8 + 8]
+    for r in range(16):
+        o_vel[:, r * 128 : (r + 1) * 128] = turned[r // 8, pl.ds(r % 8, 8, stride=8), :][0:6]
     whole(got_a, (a_send, a_recv)).wait_send()
     whole(got_b, (b_send, b_recv)).wait_send()
     for to_partner, copies in moves.values():
@@ -649,11 +675,13 @@
         pltpu.VMEM((8, 8, 128), F32),
         pltpu.VMEM((8, 8, 128), F32),
         pltpu.VMEM((12 * PARTS, 8, 8, 128), F32),
-        pltpu.VMEM((len(CHUNKS), 256, 128), jnp.bfloat16),
-        pltpu.VMEM((4, 8, 128), F32),
-        pltpu.VMEM((4, 8, 128), F32),
-        pltpu.VMEM((4, 16, 128), F32),
-        pltpu.VMEM((4, 16, 128), F32),
+        pltpu.VMEM((len(CHUNKS) - EARLY, 256, 128), jnp.bfloat16),
+        pltpu.VMEM((EARLY, 2, 128, 128), jnp.bfloat16),
+        pltpu.VMEM((128, 128), F32),
+        pltpu.VMEM((128, 128), F32),
+        pltpu.VMEM((2, 64, 128), F32),
+        pltpu.VMEM((4, 24, 128), F32),
+        pltpu.VMEM((4, 24, 128), F32),
         pltpu.VMEM((4, 16, 128), F32),
         pltpu.VMEM((4, 16, 128), F32),
         pltpu.VMEM((4, 8, 128), F32),
@@ -665,8 +693,8 @@
         pltpu.VMEM((1, 128), F32),
         pltpu.VMEM((n_gx - 1, 1, 128), F32),
         dma((18,)),
-        dma((5, 4)),
-        dma((5, 4)),
+        dma((4, 4)),
+        dma((4, 4)),
         dma((1,)),
         dma((1,)),
         dma((1,)),

time: 23.3 us -> 22.5 us (0.966)
  Pallas kernels: 22.3 us -> 21.6 us
    pallas_call x1, Pallas kernels: 21.6 us -> 20.9 us  [on_device(): pl.pallas_call(functools.partial(kernel_with_sums, n_gx, n_gy), out_shape...]
where the time goes in v3:
time: 22.5 us; the launch traced here: 22.2 us
  Pallas kernels  21.6 us (96%)
  between operations  0.65 us (3%)
    pallas_call x1, Pallas kernels, on_device(): pl.pallas_call(functools.partial(kernel_with_sums, n_gx, n_gy), out_shape...  20.9 us
    pallas_call x1, Pallas kernels, on_device(): pl.pallas_call(hand_out, out_shape=tuple((jax.ShapeDtypeStruct(shape, F32...  0.66 us

profile of v3, /device:TPU:1, one launch (start us, length us, event | category | flops | bytes accessed | tf_op | source)
XLA Modules:
  0.0 22.2 jit_solution(12310056813456424168)
XLA Ops:
  0.6 20.9 %shard_map.193 = (f32[6,2048]{1,0:T(8,128)S(1)}, f32[20,128]{1,0:T(8,128)S(1)}, f32[4,256]{1,0:T(4,128)S(1)}) custom-call(f32[3,2048]{1,0:T(4,128)} %refs_0_.1, f32[16,128]{1,0:T(8,128)} %bitcast.21, f32[16,128]{1,0:T(8,128)} %bitcast.22, f32[16,128]{1,0:T(8,128)} %bitcast.23, f32[16,128]{1,0:T(8,128)} %bitcast.24, f32[16,128]{1,0:T(8,128)} %bitcast.25, ...), custom_call_target="tpu_custom_call" | custom-call | tf_op jit(solution)/shard_map/pallas_call | solution.py:707
  21.6 0.7 %shard_map.194 = (f32[6,2048]{1,0:T(8,128)}, f32[20,128]{1,0:T(8,128)}, f32[4,256]{1,0:T(4,128)}) custom-call(f32[6,2048]{1,0:T(8,128)S(1)} %get-tuple-element.9.vel, f32[20,128]{1,0:T(8,128)S(1)} %get-tuple-element.10.fl, f32[4,256]{1,0:T(4,128)S(1)} %get-tuple-element.11.fc), custom_call_target="tpu_custom_call" | custom-call | tf_op jit(solution)/shard_map/pallas_call | solution.py:717

commit v4 on v3

--- a/solution.py
+++ b/solution.py
@@ -108,15 +108,11 @@
     recv_g,
     sum_a,
     got_a,
-    sum_b,
-    got_b,
     in_sem,
     ex_send,
     ex_recv,
     a_send,
     a_recv,
-    b_send,
-    b_recv,
     relay,
     wide_0,
     wide_1,
@@ -307,8 +303,8 @@
         for d in range(4):
             send_d[d, 2 * i : 2 * i + 2, :] = value[2 * d : 2 * d + 2]
     pl.semaphore_wait(barrier, greetings)
-    for o in range(1, n_z):
-        pl.semaphore_signal(relay.at[0], inc=1, device_id=plane(0, o), device_id_type=MESH)
+    for o in range(1, n_y):
+        pl.semaphore_signal(relay.at[0], inc=1, device_id=plane(o, 0), device_id_type=MESH)
 
     launch(send_e, recv_e, 0, False)
     launch(send_d, recv_d, 1, True)
@@ -459,6 +455,9 @@
     both_units = (wide_0, wide_1)
     accumulate(both_units, 0, [loads_from(chunk, wide) for chunk in CHUNKS[:LOCAL_CHUNKS]])
 
+    pl.semaphore_wait(relay.at[0], n_y - 1)
+    for o in range(1, n_z):
+        pl.semaphore_signal(relay.at[1], inc=1, device_id=plane(0, o), device_id_type=MESH)
     arrive(0)
     arrive(1)
 
@@ -551,8 +550,17 @@
             device_id_type=MESH,
         )
 
-    for o in range(1, n_gy):
-        ring(sum_a, got_a, (a_send, a_recv), o - 1, place(0, o)).start()
+    def hops(offset):
+        o, oy, oz = offset
+        return min(o, n_gy - o) / 2 + min(oy, n_y - oy) + min(oz, n_z - oz)
+
+    others = [(o, oy, oz) for o in range(n_gy) for oy in range(n_y) for oz in range(n_z)][1:]
+    others.sort(key=hops, reverse=True)
+    columns = [lax.rem(gy + o, n_gy) for o in range(n_gy)]
+    planes = {(oy, oz): plane(oy, oz)[0] for oy in range(n_y) for oz in range(n_z)}
+    pl.semaphore_wait(relay.at[1], n_z - 1)
+    for slot, (o, oy, oz) in enumerate(others):
+        ring(sum_a, got_a, (a_send, a_recv), slot, (planes[oy, oz], columns[o])).start()
 
     def contact(e):
         values = picked(index[e], move_row, 6)
@@ -570,15 +578,6 @@
             send_g[d, 2 * c : 2 * c + 2, :] = moved_in[c][2 * d : 2 * d + 2]
     launch(send_g, recv_g, 3, False)
 
-    whole(got_a, (a_send, a_recv)).wait_recv()
-    mine = sum_a[...]
-    for o in range(1, n_gy):
-        mine = mine + got_a[o - 1]
-    sum_b[...] = mine
-    pl.semaphore_wait(relay.at[0], n_z - 1)
-    for o in range(1, n_gx):
-        ring(sum_b, got_b, (b_send, b_recv), o - 1, plane(o % n_y, o // n_y)).start()
-
     def curve(b, one, two):
         return dot3(pairs[b]["normal"], [one[c] - two[c] for c in range(3)])
 
@@ -590,10 +589,13 @@
     curved[3] = curve(3, moved_own, [repacked(recv_g, c, c) for c in range(3)])
     curved[4] = curve(4, [repacked(recv_f, c, 3 + c) for c in range(3)], moved_in)
 
-    whole(got_b, (b_send, b_recv)).wait_recv()
-    mine = sum_b[...]
-    for o in range(1, n_gx):
-        mine = mine + got_b[o - 1]
+    whole(got_a, (a_send, a_recv)).wait_recv()
+    parts = [sum_a[...]] + [got_a[slot] for slot in range(len(others))]
+    while len(parts) > 1:
+        parts = [
+            parts[i] + parts[i + 1] if i + 1 < len(parts) else parts[i] for i in range(0, len(parts), 2)
+        ]
+    mine = parts[0]
     sums = [
         jnp.sum(jnp.where(quarter == i, mine, 0.0), axis=1, keepdims=True) for i in range(4)
     ]
@@ -627,7 +629,6 @@
     for r in range(16):
         o_vel[:, r * 128 : (r + 1) * 128] = turned[r // 8, pl.ds(r % 8, 8, stride=8), :][0:6]
     whole(got_a, (a_send, a_recv)).wait_send()
-    whole(got_b, (b_send, b_recv)).wait_send()
     for to_partner, copies in moves.values():
         for d in range(4):
             pl.when(has_partner[d] if to_partner else has_owner[d])(copies[d].wait_send)
@@ -689,17 +690,13 @@
         pltpu.VMEM((4, 8, 128), F32),
         pltpu.VMEM((4, 8, 128), F32),
         pltpu.VMEM((1, 128), F32),
-        pltpu.VMEM((n_gy - 1, 1, 128), F32),
-        pltpu.VMEM((1, 128), F32),
-        pltpu.VMEM((n_gx - 1, 1, 128), F32),
+        pltpu.VMEM((n_gx * n_gy - 1, 1, 128), F32),
         dma((18,)),
         dma((4, 4)),
         dma((4, 4)),
         dma((1,)),
         dma((1,)),
-        dma((1,)),
-        dma((1,)),
-        pltpu.SemaphoreType.REGULAR((1,)),
+        pltpu.SemaphoreType.REGULAR((2,)),
     ]
     operands = [pltpu.with_memory_space_constraint(v, pltpu.HBM) for v in operands]
     outs = ((6, 2048), (20, 128), (4, 256))

time: 22.5 us -> 21.3 us (0.947)
  Pallas kernels: 21.6 us -> 20.5 us
    pallas_call x1, Pallas kernels: 20.9 us -> 19.8 us  [on_device(): pl.pallas_call(functools.partial(kernel_with_sums, n_gx, n_gy), out_shape...]
where the time goes in v4:
time: 21.3 us; the launch traced here: 21.1 us
  Pallas kernels  20.5 us (96%)
  between operations  0.65 us (3%)
    pallas_call x1, Pallas kernels, on_device(): pl.pallas_call(functools.partial(kernel_with_sums, n_gx, n_gy), out_shape...  19.8 us
    pallas_call x1, Pallas kernels, on_device(): pl.pallas_call(hand_out, out_shape=tuple((jax.ShapeDtypeStruct(shape, F32...  0.66 us

profile of v4, /device:TPU:1, one launch (start us, length us, event | category | flops | bytes accessed | tf_op | source)
XLA Modules:
  0.0 21.1 jit_solution(301329025408284237)
XLA Ops:
  0.6 19.8 %shard_map.193 = (f32[6,2048]{1,0:T(8,128)S(1)}, f32[20,128]{1,0:T(8,128)S(1)}, f32[4,256]{1,0:T(4,128)S(1)}) custom-call(f32[3,2048]{1,0:T(4,128)} %refs_0_.1, f32[16,128]{1,0:T(8,128)} %bitcast.21, f32[16,128]{1,0:T(8,128)} %bitcast.22, f32[16,128]{1,0:T(8,128)} %bitcast.23, f32[16,128]{1,0:T(8,128)} %bitcast.24, f32[16,128]{1,0:T(8,128)} %bitcast.25, ...), custom_call_target="tpu_custom_call" | custom-call | tf_op jit(solution)/shard_map/pallas_call | solution.py:704
  20.4 0.7 %shard_map.194 = (f32[6,2048]{1,0:T(8,128)}, f32[20,128]{1,0:T(8,128)}, f32[4,256]{1,0:T(4,128)}) custom-call(f32[6,2048]{1,0:T(8,128)S(1)} %get-tuple-element.9.vel, f32[20,128]{1,0:T(8,128)S(1)} %get-tuple-element.10.fl, f32[4,256]{1,0:T(4,128)S(1)} %get-tuple-element.11.fc), custom_call_target="tpu_custom_call" | custom-call | tf_op jit(solution)/shard_map/pallas_call | solution.py:714

commit v5 on v4

--- a/solution.py
+++ b/solution.py
@@ -93,7 +93,6 @@
     key_hi,
     key_lo,
     push,
-    o_mat,
     o_turned,
     key_rows,
     key_columns,
@@ -139,20 +138,13 @@
     has_partner = [inside(dx, dy) for dx, dy in OFFSETS]
     has_owner = [inside(-dx, -dy) for dx, dy in OFFSETS]
 
-    sources = (h_cent, h_tilt, h_turn, h_rad, h_perp, h_axial, h_rot, h_load, h_lf, h_ls, h_a1, h_a2, h_mine, h_slot, h_own, h_oth, h_count, h_exp)
-    targets = (v_cent, v_tilt, v_turn, v_rad, v_perp, v_axial, v_rot, v_load, v_lf, v_ls, v_a1, v_a2, v_mine, v_slot, v_own, v_oth, s_count, v_exp)
-    loads_in = {}
-    for i in (1, 2, 7, 4, 5, 6, 13, 15, 16, 17, 12, 14, 0, 3, 8, 9, 10, 11):
-        loads_in[i] = pltpu.make_async_copy(sources[i], targets[i], in_sem.at[i])
-        loads_in[i].start()
-
     barrier = pltpu.get_barrier_semaphore()
 
     def greet(to):
         pl.semaphore_signal(barrier, inc=1, device_id=to, device_id_type=MESH)
 
     greetings = (n_gy - 1) + (n_y - 1) + (n_z - 1)
-    for d in (1, 2, 3):
+    for d in (1, 3, 2):
         dx, dy = OFFSETS[d]
         pl.when(has_partner[d])(functools.partial(greet, place(dx, dy)))
         pl.when(has_owner[d])(functools.partial(greet, place(-dx, -dy)))
@@ -164,6 +156,13 @@
     for o in range(1, n_z):
         greet(plane(0, o))
 
+    sources = (h_cent, h_tilt, h_turn, h_rad, h_perp, h_axial, h_rot, h_load, h_lf, h_ls, h_a1, h_a2, h_mine, h_slot, h_own, h_oth, h_count, h_exp)
+    targets = (v_cent, v_tilt, v_turn, v_rad, v_perp, v_axial, v_rot, v_load, v_lf, v_ls, v_a1, v_a2, v_mine, v_slot, v_own, v_oth, s_count, v_exp)
+    loads_in = {}
+    for i in (1, 2, 7, 4, 5, 6, 13, 15, 16, 17, 12, 14, 0, 3, 8, 9, 10, 11):
+        loads_in[i] = pltpu.make_async_copy(sources[i], targets[i], in_sem.at[i])
+        loads_in[i].start()
+
     def need(*which):
         for i in which:
             loads_in[i].wait()
@@ -207,8 +206,8 @@
     for d in range(4):
         for h in range(2):
             piece = slice(h * 128, (h + 1) * 128)
-            send_d[d, 16 + h : 17 + h, :] = v_slot[d : d + 1, piece].astype(F32)
-            send_d[d, 18 + h : 19 + h, :] = v_oth[d : d + 1, piece]
+            send_d[d, 14 + h : 15 + h, :] = v_slot[d : d + 1, piece].astype(F32)
+            send_d[d, 16 + h : 17 + h, :] = v_oth[d : d + 1, piece]
     live_own = zero8
     for d in range(4):
         bound = s_count[0, d]
@@ -216,7 +215,7 @@
             (heading8 == d) & ((row8 - 2 * d) * 128 + lane8 < bound), 1.0, live_own
         )
     for d in range(4):
-        send_d[d, 20:22, :] = live_own[2 * d : 2 * d + 2]
+        send_d[d, 18:20, :] = live_own[2 * d : 2 * d + 2]
 
     def blank(refs, d):
         for ref in refs:
@@ -231,8 +230,8 @@
     moves = {}
 
     def launch(src, dst, step, to_partner):
-        moves[step] = to_partner, []
-        for d in range(4):
+        moves[step] = to_partner, {}
+        for d in (1, 3, 2, 0):
             copy = pltpu.make_async_remote_copy(
                 src_ref=src.at[d],
                 dst_ref=dst.at[d],
@@ -241,7 +240,7 @@
                 device_id=partner[d] if to_partner else owner[d],
                 device_id_type=MESH,
             )
-            moves[step][1].append(copy)
+            moves[step][1][d] = copy
             pl.when(has_partner[d] if to_partner else has_owner[d])(copy.start)
 
     def arrive(step):
@@ -338,9 +337,6 @@
     def tall_row(first, second):
         return jnp.concatenate([first, second], axis=0).astype(jnp.bfloat16)
 
-    low = [
-        tall_row(row8.astype(F32) + float(k), row8.astype(F32) + float(k + 8)) for k in range(0, 256, 16)
-    ]
     high = tall_row(row8.astype(F32), row8.astype(F32))
     one16 = jnp.ones((16, 128), jnp.bfloat16)
     none16 = jnp.zeros((16, 128), jnp.bfloat16)
@@ -362,20 +358,18 @@
         for n, (e, s) in enumerate(CHUNKS[:EARLY]):
             key_rows[n : n + 1, :] = key_lo[e, s : s + 1, :]
         key_rows[EARLY:, :] = jnp.zeros((128 - EARLY, 128), F32)
-        key_columns[...] = jnp.transpose(key_rows[...])
+        key_columns[0] = jnp.transpose(key_rows[...])
+
+    def turn_late_keys():
+        key_columns[1, :, 0:8] = jnp.transpose(key_lo[7])
 
     def set_columns(n):
-        if n < EARLY:
-            for k in range(0, 128, 16):
-                key = jnp.broadcast_to(key_columns[k : k + 16, n : n + 1], (16, 128)).astype(jnp.bfloat16)
-                for h in range(2):
-                    o_turned[n, h, k : k + 16, :] = jnp.where(lanes[h] == key, one16, none16)
-            return
-        e, s = CHUNKS[n]
-        key = spread_rows(key_lo, s, e)
-        key = tall_row(key, key)
-        for k in range(0, 256, 16):
-            o_mat[n - EARLY, k : k + 16, :] = jnp.where(low[k // 16] == key, one16, none16)
+        late, at = n // EARLY, n % EARLY
+        for k in range(0, 128, 16):
+            key = key_columns[late, k : k + 16, at : at + 1]
+            key = jnp.broadcast_to(key, (16, 128)).astype(jnp.bfloat16)
+            for h in range(2):
+                o_turned[n, h, k : k + 16, :] = jnp.where(lanes[h] == key, one16, none16)
 
     def columns_beside(first, last, every):
         for n in range(first, last):
@@ -392,24 +386,28 @@
             out.append(jnp.where(here, value, none16))
         return out
 
-    def accumulate(into, start, rows):
-        for n in range(0, len(rows), 2):
-            unit = (start + n) // 2 % 2
-            stage = (start + n) // 4 % 2
-            if start + n < EARLY:
-                tile = [
-                    jnp.concatenate([o_turned[at, 0], o_turned[at, 1]], axis=1)
-                    for at in (start + n, start + n + 1)
-                ]
-                tile = jnp.concatenate(tile, axis=0)
-            else:
-                at = start + n - EARLY
-                tile = jnp.concatenate([o_mat[at], o_mat[at + 1]], axis=1)
-            pltpu.matmul_push_rhs(
-                tile, staging_register=stage, mxu_index=unit, transpose=start + n >= EARLY
+    slices = len(CHUNKS) // 2
+
+    def push_tile(g):
+        n = 2 * g
+        tile = [jnp.concatenate([o_turned[at, 0], o_turned[at, 1]], axis=1) for at in (n, n + 1)]
+        pltpu.matmul_push_rhs(
+            jnp.concatenate(tile, axis=0), staging_register=g // 2 % 2, mxu_index=g % 2
+        )
+
+    def first_tiles():
+        for g in range(4):
+            push_tile(g)
+
+    def accumulate(into, first, rows):
+        for i in range(0, len(rows), 2):
+            g = first + i // 2
+            left = [jnp.concatenate(r, axis=0) for r in rows[i : i + 2]]
+            pltpu.matmul_acc_lhs(
+                into[g % 2], jnp.concatenate(left, axis=1), load_staged_rhs=g // 2 % 2
             )
-            left = [jnp.concatenate(r, axis=0) for r in rows[n : n + 2]]
-            pltpu.matmul_acc_lhs(into[unit], jnp.concatenate(left, axis=1), load_staged_rhs=stage)
+            if g + 4 < slices:
+                push_tile(g + 4)
 
     def total_of(into):
         return pltpu.matmul_pop(into[0]) + pltpu.matmul_pop(into[1])
@@ -453,6 +451,7 @@
     for b in range(3):
         set_ends(b, b, 3 + b, (pairs[b]["slope"], pairs[b]["down"]))
     both_units = (wide_0, wide_1)
+    first_tiles()
     accumulate(both_units, 0, [loads_from(chunk, wide) for chunk in CHUNKS[:LOCAL_CHUNKS]])
 
     pl.semaphore_wait(relay.at[0], n_y - 1)
@@ -472,13 +471,19 @@
             out = jnp.where(heading8 == d, row_of(d), out)
         return out
 
-    slot_in = repacked(recv_d, 8, 2).astype(I32)
-    arc_in = repacked(recv_d, 9, 3)
-    live_in = repacked(recv_d, 10, 4)
+    slot_in = repacked(recv_d, 7, 2).astype(I32)
+    arc_in = repacked(recv_d, 8, 3)
+    live_in = repacked(recv_d, 9, 4)
     index[7] = lanes_of(by_heading(lambda d: spread_rows(v_exp, d)), slot_in)
     set_keys(7)
+    turn_late_keys()
     columns_beside(EARLY, len(CHUNKS), 2)
-    ends[7] = endpoint(picked(index[7], table_row, 13), arc_in)
+    offered_here = [
+        lanes_of(by_heading(lambda d, c=c: spread_rows(send_e, c, d)), slot_in) for c in range(13)
+    ]
+    ends[7] = endpoint(offered_here, arc_in)
+    while beside:
+        beside.pop(0)()
 
     slot_own = unpacked(v_slot, pk_int, 1)
     arc_oth = unpacked(v_oth, pk, 6)
@@ -494,7 +499,7 @@
     pairs[4] = pair(dict(at=near[0:3], radius=near[3], moving=near[4:7]), ends[7], live_in)
     set_ends(4, None, 7, (pairs[4]["slope"], pairs[4]["down"]))
 
-    accumulate(both_units, LOCAL_CHUNKS, [loads_from(chunk, wide) for chunk in CHUNKS[LOCAL_CHUNKS:]])
+    accumulate(both_units, LOCAL_CHUNKS // 2, [loads_from(chunk, wide) for chunk in CHUNKS[LOCAL_CHUNKS:]])
     total = total_of(both_units)
     both = loads_of(total, 0) + loads_of(total, 1)
     moved_all = mobile(both[0:6])
@@ -589,6 +594,7 @@
     curved[3] = curve(3, moved_own, [repacked(recv_g, c, c) for c in range(3)])
     curved[4] = curve(4, [repacked(recv_f, c, 3 + c) for c in range(3)], moved_in)
 
+    first_tiles()
     whole(got_a, (a_send, a_recv)).wait_recv()
     parts = [sum_a[...]] + [got_a[slot] for slot in range(len(others))]
     while len(parts) > 1:
@@ -676,19 +682,18 @@
         pltpu.VMEM((8, 8, 128), F32),
         pltpu.VMEM((8, 8, 128), F32),
         pltpu.VMEM((12 * PARTS, 8, 8, 128), F32),
-        pltpu.VMEM((len(CHUNKS) - EARLY, 256, 128), jnp.bfloat16),
-        pltpu.VMEM((EARLY, 2, 128, 128), jnp.bfloat16),
+        pltpu.VMEM((len(CHUNKS), 2, 128, 128), jnp.bfloat16),
         pltpu.VMEM((128, 128), F32),
-        pltpu.VMEM((128, 128), F32),
+        pltpu.VMEM((2, 128, 128), F32),
         pltpu.VMEM((2, 64, 128), F32),
-        pltpu.VMEM((4, 24, 128), F32),
-        pltpu.VMEM((4, 24, 128), F32),
-        pltpu.VMEM((4, 16, 128), F32),
-        pltpu.VMEM((4, 16, 128), F32),
-        pltpu.VMEM((4, 8, 128), F32),
-        pltpu.VMEM((4, 8, 128), F32),
-        pltpu.VMEM((4, 8, 128), F32),
-        pltpu.VMEM((4, 8, 128), F32),
+        pltpu.VMEM((4, 20, 128), F32),
+        pltpu.VMEM((4, 20, 128), F32),
+        pltpu.VMEM((4, 13, 128), F32),
+        pltpu.VMEM((4, 13, 128), F32),
+        pltpu.VMEM((4, 6, 128), F32),
+        pltpu.VMEM((4, 6, 128), F32),
+        pltpu.VMEM((4, 6, 128), F32),
+        pltpu.VMEM((4, 6, 128), F32),
         pltpu.VMEM((1, 128), F32),
         pltpu.VMEM((n_gx * n_gy - 1, 1, 128), F32),
         dma((18,)),

time: 21.3 us -> 21.1 us (level)
  no operation moved by 1% of the time
where the time goes in v5:
time: 21.1 us; the launch traced here: 20.9 us
  Pallas kernels  20.3 us (96%)
  between operations  0.65 us (3%)
    pallas_call x1, Pallas kernels, on_device(): pl.pallas_call(functools.partial(kernel_with_sums, n_gx, n_gy), out_shape...  19.6 us
    pallas_call x1, Pallas kernels, on_device(): pl.pallas_call(hand_out, out_shape=tuple((jax.ShapeDtypeStruct(shape, F32...  0.66 us

profile of v5, /device:TPU:1, one launch (start us, length us, event | category | flops | bytes accessed | tf_op | source)
XLA Modules:
  0.0 20.9 jit_solution(6063219030902120825)
XLA Ops:
  0.6 19.6 %shard_map.193 = (f32[6,2048]{1,0:T(8,128)S(1)}, f32[20,128]{1,0:T(8,128)S(1)}, f32[4,256]{1,0:T(4,128)S(1)}) custom-call(f32[3,2048]{1,0:T(4,128)} %refs_0_.1, f32[16,128]{1,0:T(8,128)} %bitcast.21, f32[16,128]{1,0:T(8,128)} %bitcast.22, f32[16,128]{1,0:T(8,128)} %bitcast.23, f32[16,128]{1,0:T(8,128)} %bitcast.24, f32[16,128]{1,0:T(8,128)} %bitcast.25, ...), custom_call_target="tpu_custom_call" | custom-call | tf_op jit(solution)/shard_map/pallas_call | solution.py:709
  20.3 0.7 %shard_map.194 = (f32[6,2048]{1,0:T(8,128)}, f32[20,128]{1,0:T(8,128)}, f32[4,256]{1,0:T(4,128)}) custom-call(f32[6,2048]{1,0:T(8,128)S(1)} %get-tuple-element.9.vel, f32[20,128]{1,0:T(8,128)S(1)} %get-tuple-element.10.fl, f32[4,256]{1,0:T(4,128)S(1)} %get-tuple-element.11.fc), custom_call_target="tpu_custom_call" | custom-call | tf_op jit(solution)/shard_map/pallas_call | solution.py:719

commit v6 on v5

--- a/solution.py
+++ b/solution.py
@@ -557,7 +557,7 @@
 
     def hops(offset):
         o, oy, oz = offset
-        return min(o, n_gy - o) / 2 + min(oy, n_y - oy) + min(oz, n_z - oz)
+        return (min(o, n_gy - o) + 1) // 2 + min(oy, n_y - oy) + min(oz, n_z - oz)
 
     others = [(o, oy, oz) for o in range(n_gy) for oy in range(n_y) for oz in range(n_z)][1:]
     others.sort(key=hops, reverse=True)

time: 21.1 us -> 21.1 us (level)
  no operation moved by 1% of the time
where the time goes in v6:
time: 21.1 us; the launch traced here: 20.9 us
  Pallas kernels  20.3 us (96%)
  between operations  0.65 us (3%)
    pallas_call x1, Pallas kernels, on_device(): pl.pallas_call(functools.partial(kernel_with_sums, n_gx, n_gy), out_shape...  19.6 us
    pallas_call x1, Pallas kernels, on_device(): pl.pallas_call(hand_out, out_shape=tuple((jax.ShapeDtypeStruct(shape, F32...  0.66 us

profile of v6, /device:TPU:1, one launch (start us, length us, event | category | flops | bytes accessed | tf_op | source)
XLA Modules:
  0.0 20.9 jit_solution(4153335170328662396)
XLA Ops:
  0.6 19.6 %shard_map.193 = (f32[6,2048]{1,0:T(8,128)S(1)}, f32[20,128]{1,0:T(8,128)S(1)}, f32[4,256]{1,0:T(4,128)S(1)}) custom-call(f32[3,2048]{1,0:T(4,128)} %refs_0_.1, f32[16,128]{1,0:T(8,128)} %bitcast.21, f32[16,128]{1,0:T(8,128)} %bitcast.22, f32[16,128]{1,0:T(8,128)} %bitcast.23, f32[16,128]{1,0:T(8,128)} %bitcast.24, f32[16,128]{1,0:T(8,128)} %bitcast.25, ...), custom_call_target="tpu_custom_call" | custom-call | tf_op jit(solution)/shard_map/pallas_call | solution.py:709
  20.3 0.7 %shard_map.194 = (f32[6,2048]{1,0:T(8,128)}, f32[20,128]{1,0:T(8,128)}, f32[4,256]{1,0:T(4,128)}) custom-call(f32[6,2048]{1,0:T(8,128)S(1)} %get-tuple-element.9.vel, f32[20,128]{1,0:T(8,128)S(1)} %get-tuple-element.10.fl, f32[4,256]{1,0:T(4,128)S(1)} %get-tuple-element.11.fc), custom_call_target="tpu_custom_call" | custom-call | tf_op jit(solution)/shard_map/pallas_call | solution.py:719
